TPU v7x, 32 devices: a whole 2x2x4 slice. The times are simulated.
32 devices in a mesh: lat: 8 (over z, core), lon: 4 (over y, x).
Axes of the slice: x: 2, y: 2, z: 4, core: 2. Of those that a mesh axis runs over, the one named last changes fastest.
Arguments:
- pedersen: float32 [16, 1024, 2048], P(None, 'lat', 'lon'), may hold values from 0.2 to 2
- hall_conductivity: float32 [16, 1024, 2048], P(None, 'lat', 'lon'), may hold values from 0.1 to 1.5
- east_wind: float32 [16, 1024, 2048], P(None, 'lat', 'lon'), may hold values from -6 to 6
- north_wind: float32 [16, 1024, 2048], P(None, 'lat', 'lon'), may hold values from -6 to 6
- ion_density: float32 [3, 1024, 2048], P(None, 'lat', 'lon'), may hold values from 0.5 to 2
Outputs:
- potential: float32 [1024, 2048], P('lat', 'lon')
- ion_update: float32 [3, 1024, 2048], P(None, 'lat', 'lon')
All inputs are finite; a program needn't handle non-finite values. Where the computation divides by a largest or mean magnitude, that divisor is 1e-20 or more.
Results may differ from a plain program's by a relative error of at most 0.00002.
Values sent between devices are 32-bit elements; how exact they have to be, the bound alone decides.
A program may use at most 192 MiB of HBM per device.

v0:
```python
import jax
import jax.numpy as jnp
from jax import lax
from jax.sharding import PartitionSpec as P

LEV = 16
SWEEPS = 16


DAMPING = 0.0001
LOW_BOUND = 0.05
HIGH_BOUND = 2.0
COURANT = 0.8
MOBILITY = (1.0, 0.6, 0.3)
NEIGHBOURS = (
    (-1, 0, 1.0),
    (1, 0, 1.0),
    (0, -1, 1.0),
    (0, 1, 1.0),
    (-1, -1, 0.5),
    (-1, 1, 0.5),
    (1, -1, 0.5),
    (1, 1, 0.5),
)


def swapped(array, axis, bit):
    return lax.ppermute(array, axis, [(i, i ^ 1 << bit) for i in range(lax.axis_size(axis))])


def padded(array, sides, width):
    for axis, dim in sides:
        peers, length = (lax.axis_size(axis), array.shape[dim])
        up = [(i, (i + 1) % peers) for i in range(peers)]
        down = [(j, i) for i, j in up]
        last = lax.slice_in_dim(array, length - width, length, axis=dim)
        initial = lax.slice_in_dim(array, 0, width, axis=dim)
        before = lax.ppermute(last, axis, up)
        after = lax.ppermute(initial, axis, down)
        array = jnp.concatenate([before, array, after], axis=dim)
    return array


def thickness():
    levels = jnp.arange(LEV, dtype=jnp.float32)
    return (0.5 + levels / LEV) / LEV


def chebyshev_factors():
    theta = 0.5 * (HIGH_BOUND + LOW_BOUND)
    delta = 0.5 * (HIGH_BOUND - LOW_BOUND)
    sigma_one = theta / delta
    rho_prev = 1.0 / sigma_one
    first_list = []
    second_list = []
    for sweep in range(SWEEPS):
        rho_next = 1.0 / (2.0 * sigma_one - rho_prev)
        first_list.append(rho_next * rho_prev)
        second_list.append(2.0 * rho_next / delta)
        rho_prev = rho_next
    return (theta, first_list, second_list)


def window(array, shift_lat, shift_lon):
    height = array.shape[0] - 2
    breadth = array.shape[1] - 2
    return array[1 + shift_lat : 1 + shift_lat + height, 1 + shift_lon : 1 + shift_lon + breadth]


def stencil(sigma_ext):
    center = window(sigma_ext, 0, 0)
    weights = []
    diagonal = jnp.zeros_like(center) + DAMPING
    for shift_lat, shift_lon, factor in NEIGHBOURS:
        weight = factor * 0.5 * (center + window(sigma_ext, shift_lat, shift_lon))
        weights.append(weight)
    for weight in weights:
        diagonal = diagonal + weight
    return (weights, diagonal)


def apply_operator(field_ext, weights, diagonal):
    result = diagonal * window(field_ext, 0, 0)
    for index_pair, (shift_lat, shift_lon, factor) in enumerate(NEIGHBOURS):
        result = result - weights[index_pair] * window(field_ext, shift_lat, shift_lon)
    return result


def divergence(east_ext, north_ext):
    return 0.5 * (window(east_ext, 0, 1) - window(east_ext, 0, -1)) + 0.5 * (
        window(north_ext, 1, 0) - window(north_ext, -1, 0)
    )


def advect(density_ext, cross_east, cross_north):
    density = window(density_ext, 0, 0)
    result = density - jnp.maximum(cross_east, 0.0) * (density - window(density_ext, 0, -1))
    result = result - jnp.minimum(cross_east, 0.0) * (window(density_ext, 0, 1) - density)
    result = result - jnp.maximum(cross_north, 0.0) * (density - window(density_ext, -1, 0))
    result = result - jnp.minimum(cross_north, 0.0) * (window(density_ext, 1, 0) - density)
    return result


def shards(pedersen, hall_conductivity, east_wind, north_wind, ion_density):
    lat_rows = pedersen.shape[1]
    lon_cells = pedersen.shape[2]
    lat_total = lat_rows * lax.axis_size("lat")
    band_index = lax.axis_index("lat")

    def inside(width):
        global_rows = (
            band_index * lat_rows - width + jnp.arange(lat_rows + 2 * width, dtype=jnp.int32)
        )
        return jnp.where((global_rows >= 0) & (global_rows < lat_total), 1.0, 0.0).astype(
            jnp.float32
        )[:, None]

    layer = thickness()[:, None, None]
    sigma = jnp.sum(layer * pedersen, 0)
    current_east = jnp.sum(layer * (pedersen * east_wind + hall_conductivity * north_wind), 0)
    current_north = jnp.sum(layer * (pedersen * north_wind - hall_conductivity * east_wind), 0)
    stacked = jnp.stack([sigma, current_east, current_north])
    mirrored = stacked[:, ::-1, :]
    for bit_number in range(lax.axis_size("lat").bit_length() - 1):
        mirrored = swapped(mirrored, "lat", bit_number)
    combined = stacked + mirrored
    depth = 1
    reach = depth + 1
    drivers = padded(combined, (("lat", 1), ("lon", 2)), reach)
    drivers = drivers * inside(reach)[None]
    weights, diagonal = stencil(drivers[0])
    source = divergence(drivers[1], drivers[2])
    mask_inner = inside(depth)
    theta, first_list, second_list = chebyshev_factors()
    first_table = jnp.array(first_list, jnp.float32)
    second_table = jnp.array(second_list, jnp.float32)

    def crop(array):
        return array[depth : depth + lat_rows, depth : depth + lon_cells]

    solution = jnp.zeros((lat_rows, lon_cells), jnp.float32)
    update = crop(source / diagonal / theta)

    def group(group_index, carry):
        state = jnp.stack([carry[0], carry[1]])
        state_ext = padded(state, (("lat", 1), ("lon", 2)), depth)
        solution_ext = state_ext[0] * mask_inner
        update_ext = state_ext[1] * mask_inner
        position = group_index * depth + 0
        solution_ext = solution_ext + update_ext
        image = apply_operator(jnp.pad(solution_ext, 1), weights, diagonal)
        scaled = mask_inner * ((source - image) / diagonal)
        update_ext = first_table[position] * update_ext + second_table[position] * scaled
        return (crop(solution_ext), crop(update_ext))

    solution, update = lax.fori_loop(0, SWEEPS // depth, group, (solution, update))
    fields = jnp.concatenate([solution[None], ion_density], 0)
    fields_ext = padded(fields, (("lat", 1), ("lon", 2)), 1)
    fields_ext = fields_ext * inside(1)[None]
    potential_ext = fields_ext[0]
    drift_east = -0.5 * (window(potential_ext, 1, 0) - window(potential_ext, -1, 0))
    drift_north = 0.5 * (window(potential_ext, 0, 1) - window(potential_ext, 0, -1))
    fastest = lax.pmax(jnp.max(jnp.abs(drift_east) + jnp.abs(drift_north)), ("lat", "lon"))
    time_step = COURANT / (fastest + 1e-06)
    results = []
    for species in range(3):
        cross_east = MOBILITY[species] * time_step * drift_east
        cross_north = MOBILITY[species] * time_step * drift_north
        results.append(advect(fields_ext[species + 1], cross_east, cross_north))
    return (solution, jnp.stack(results))


def solution(mesh):
    in_specs = (
        P(None, "lat", "lon"),
        P(None, "lat", "lon"),
        P(None, "lat", "lon"),
        P(None, "lat", "lon"),
        P(None, "lat", "lon"),
    )
    out_specs = (P("lat", "lon"), P(None, "lat", "lon"))
    return jax.shard_map(shards, mesh=mesh, in_specs=in_specs, out_specs=out_specs, check_vma=False)
```

profile of v0, /device:TPU:0, one launch (start us, length us, event | category | flops | bytes accessed | tf_op | source)
XLA Modules:
  0.0 441.9 jit_solution(17320150490575766264)
XLA Ops:
  0.6 7.1 %multiply_reduce_fusion.1 = (f32[128,512]{1,0:T(8,128)S(1)}, f32[128,512]{1,0:T(8,128)S(1)}, f32[128,512]{1,0:T(8,128)S(1)}) fusion(f32[16,128,512]{2,1,0:T(8,128)} %param.10, f32[16,128,512]{2,1,0:T(8,128)} %param.12, f32[16,128,512]{2,1,0:T(8,128)} %param.9, f32[16,128,512]{2,1,0:T(8,128)} %param.11, f32[16]{0:T(128)S(1)} %add_multiply_fusion), kind=kLoop, calls=%fused_computation.24 | loop fusion | flops 12386304 | bytes 17563712 | tf_op jit(solution)/shard_map/reduce_sum | solution.py:120
  8.8 1.9 collective-permute-done.4
  10.7 2.9 collective-permute-start.5
  13.6 17.8 %collective-permute-done.5 = f32[3,128,512]{2,1,0:T(8,128)S(1)} collective-permute-done((f32[3,128,512]{2,1,0:T(8,128)S(1)}, f32[3,128,512]{2,1,0:T(8,128)S(1)}, u32[]{:S(2)}, u32[]{:S(2)}) %collective-permute-start.5) | collective-permute-done | bytes 786464 | tf_op jit(solution)/shard_map/ppermute | solution.py:28
  31.5 2.8 collective-permute-start.6
  34.2 34.0 %collective-permute-done.6 = f32[3,128,512]{2,1,0:T(8,128)S(1)} collective-permute-done((f32[3,128,512]{2,1,0:T(8,128)S(1)}, f32[3,128,512]{2,1,0:T(8,128)S(1)}, u32[]{:S(2)}, u32[]{:S(2)}) %collective-permute-start.6) | collective-permute-done | bytes 786464 | tf_op jit(solution)/shard_map/ppermute | solution.py:28
  68.5 3.5 collective-permute-start.8
  73.6 2.4 collective-permute-start.10
  76.0 5.7 %collective-permute-done.10 = f32[3,132,2]{2,1,0:T(8,128)S(1)} collective-permute-done((f32[3,132,2]{2,1,0:T(8,128)S(1)}, f32[3,132,2]{2,1,0:T(8,128)S(1)}, u32[]{:S(2)}, u32[]{:S(2)}) %collective-permute-start.10) | collective-permute-done | bytes 3200 | tf_op jit(solution)/shard_map/ppermute | solution.py:39
  81.6 3.6 collective-permute-done.9
  88.2 291.3 %while.19 = (s32[]{:T(128)}, f32[128,512]{1,0:T(8,128)S(1)}, f32[128,512]{1,0:T(8,128)S(1)}, f32[130,514]{1,0:T(8,128)S(1)}, f32[130,514]{1,0:T(8,128)S(1)}, /*i...) while((s32[]{:T(128)}, f32[128,512]{1,0:T(8,128)S(1)}, ...), condition=%wide.region_4.5_spmd.clone.clone, body=%wide.region_3.4_spmd.sunk.clone.clone.sunk | while | flops 2400792 | bytes 9622957 | solution.py:156
  88.2 2.9 collective-permute-start
  92.4 3.5 collective-permute-done.1
  100.1 1.9 collective-permute-done.2
  102.0 2.4 collective-permute-done.3
  107.6 1.7 fusion.59
  110.7 3.6 collective-permute-done.1
  115.1 1.8 collective-permute-start.2
  118.4 1.9 collective-permute-done.2
  120.4 2.8 collective-permute-done.3
  129.4 3.6 collective-permute-done.1
  137.1 1.9 collective-permute-done.2
  143.7 1.7 fusion.59
  146.9 3.6 collective-permute-done.1
  154.6 1.9 collective-permute-done.2
  156.5 2.6 collective-permute-done.3
  165.4 3.6 collective-permute-done.1
  173.1 1.9 collective-permute-done.2
  182.8 3.6 collective-permute-done.1
  190.5 1.9 collective-permute-done.2
  192.4 2.6 collective-permute-done.3
  201.3 3.6 collective-permute-done.1
  209.0 1.9 collective-permute-done.2
  218.7 3.6 collective-permute-done.1
  226.4 1.9 collective-permute-done.2
  228.4 2.6 collective-permute-done.3
  237.2 3.6 collective-permute-done.1
  244.9 1.9 collective-permute-done.2
  254.7 3.6 collective-permute-done.1
  262.4 1.9 collective-permute-done.2
  264.3 2.6 collective-permute-done.3
  270.0 1.7 fusion.59
  273.1 3.6 collective-permute-done.1
  280.8 1.9 collective-permute-done.2
  290.6 3.6 collective-permute-done.1
  298.3 1.9 collective-permute-done.2
  300.2 2.6 collective-permute-done.3
  309.1 3.6 collective-permute-done.1
  316.8 1.9 collective-permute-done.2
  323.4 1.7 fusion.59
  326.5 3.6 collective-permute-done.1
  334.2 1.9 collective-permute-done.2
  336.2 2.6 collective-permute-done.3
  345.0 3.6 collective-permute-done.1
  352.7 1.9 collective-permute-done.2
  362.5 3.6 collective-permute-done.1
  370.2 1.9 collective-permute-done.2
  372.1 2.6 collective-permute-done.3
  377.8 1.7 fusion.59
  380.5 3.5 collective-permute-start.12
  387.3 2.3 collective-permute-start.14
  389.6 6.3 %collective-permute-done.13 = f32[4,130,1]{2,1,0:T(8,128)S(1)} collective-permute-done((f32[4,130,1]{2,1,0:T(8,128)S(1)}, f32[4,130,1]{2,1,0:T(8,128)S(1)}, u32[]{:S(2)}, u32[]{:S(2)}) %collective-permute-start.13) | collective-permute-done | bytes 2112 | tf_op jit(solution)/shard_map/ppermute | solution.py:38
  396.0 2.0 collective-permute-done.14
  400.7 38.6 %pmax.7 = f32[]{:T(128)} all-reduce(f32[]{:T(128)} %get-tuple-element.486), channel_id=1, replica_groups=mesh['lat'=8,'lon'=4] {'lat','lon'}, use_global_device_ids=true, to_apply=%region_6.7 | all-reduce | flops 1 | bytes 8 | tf_op jit(solution)/shard_map/pmax | solution.py:163
  (326 shorter events, 180.6 us)
Async XLA Ops:
  8.2 2.5 collective-permute-start.4
  10.7 20.8 %collective-permute-start.5 = (f32[3,128,512]{2,1,0:T(8,128)S(1)}, f32[3,128,512]{2,1,0:T(8,128)S(1)}, u32[]{:S(2)}, u32[]{:S(2)}) collective-permute-start(f32[3,128,512]{2,1,0:T(8,128)S(1)} %collective-permute-done.4), channel_id=1, source_target_pairs={{0,8},{4,12},{8,0},{12,4},{16,24},{20,28},{24,16},{28,20},{1,9},{5... | collective-permute-start | bytes 2359304 | tf_op jit(solution)/shard_map/ppermute | solution.py:28
  31.5 36.8 %collective-permute-start.6 = (f32[3,128,512]{2,1,0:T(8,128)S(1)}, f32[3,128,512]{2,1,0:T(8,128)S(1)}, u32[]{:S(2)}, u32[]{:S(2)}) collective-permute-start(f32[3,128,512]{2,1,0:T(8,128)S(1)} %collective-permute-done.5), channel_id=1, source_target_pairs={{0,16},{4,20},{8,24},{12,28},{16,0},{20,4},{24,8},{28,12},{1,17},{... | collective-permute-start | bytes 2359304 | tf_op jit(solution)/shard_map/ppermute | solution.py:28
  68.4 5.0 %collective-permute-start.7 = (f32[3,2,512]{2,1,0:T(2,128)S(1)}, f32[3,2,512]{2,1,0:T(2,128)S(1)}, u32[]{:S(2)}, u32[]{:S(2)}) collective-permute-start(f32[3,2,512]{2,1,0:T(2,128)S(1)} %get-tuple-element.519), channel_id=1, source_target_pairs={{0,4},{4,8},{8,12},{12,16},{16,20},{20,24},{24,28},{28,0},{1,5},{5... | collective-permute-start | bytes 36872 | tf_op jit(solution)/shard_map/ppermute | solution.py:38
  68.5 4.9 %collective-permute-start.8 = (f32[3,2,512]{2,1,0:T(2,128)S(1)}, f32[3,2,512]{2,1,0:T(2,128)S(1)}, u32[]{:S(2)}, u32[]{:S(2)}) collective-permute-start(f32[3,2,512]{2,1,0:T(2,128)S(1)} %get-tuple-element.520), channel_id=1, source_target_pairs={{4,0},{8,4},{12,8},{16,12},{20,16},{24,20},{28,24},{0,28},{5,1},{9... | collective-permute-start | bytes 36872 | tf_op jit(solution)/shard_map/ppermute | solution.py:39
  73.6 8.1 %collective-permute-start.10 = (f32[3,132,2]{2,1,0:T(8,128)S(1)}, f32[3,132,2]{2,1,0:T(8,128)S(1)}, u32[]{:S(2)}, u32[]{:S(2)}) collective-permute-start(f32[3,132,2]{2,1,0:T(8,128)S(1)} %get-tuple-element.518), channel_id=1, source_target_pairs={{1,0},{2,1},{3,2},{0,3},{5,4},{6,5},{7,6},{4,7},{9,8},{10,9},{11,1... | collective-permute-start | bytes 9512 | tf_op jit(solution)/shard_map/ppermute | solution.py:39
  75.9 9.3 %collective-permute-start.9 = (f32[3,132,2]{2,1,0:T(8,128)S(1)}, f32[3,132,2]{2,1,0:T(8,128)S(1)}, u32[]{:S(2)}, u32[]{:S(2)}) collective-permute-start(f32[3,132,2]{2,1,0:T(8,128)S(1)} %get-tuple-element.517), channel_id=1, source_target_pairs={{0,1},{1,2},{2,3},{3,0},{4,5},{5,6},{6,7},{7,4},{8,9},{9,10},{10,1... | collective-permute-start | bytes 9512 | tf_op jit(solution)/shard_map/ppermute | solution.py:38
  88.2 4.2 collective-permute-start
  91.1 4.8 %collective-permute-start.1 = (f32[2,1,512]{2,1,0:T(1,128)S(1)}, f32[2,1,512]{2,1,0:T(1,128)S(1)}, u32[]{:S(2)}, u32[]{:S(2)}) collective-permute-start(f32[2,1,512]{2,1,0:T(1,128)S(1)} %get-tuple-element.618), channel_id=1, source_target_pairs={{0,4},{4,8},{8,12},{12,16},{16,20},{20,24},{24,28},{28,0},{1,5},{5... | collective-permute-start | bytes 12296 | tf_op jit(solution)/shard_map/while/body/eval_jaxpr/ppermute | solution.py:38
  96.7 5.3 %collective-permute-start.2 = (f32[2,130,1]{2,1,0:T(8,128)}, f32[2,130,1]{2,1,0:T(8,128)S(1)}, u32[]{:S(2)}, u32[]{:S(2)}) collective-permute-start(f32[2,130,1]{2,1,0:T(8,128)} %get-tuple-element.619), channel_id=1, source_target_pairs={{1,0},{2,1},{3,2},{0,3},{5,4},{6,5},{7,6},{4,7},{9,8},{10,9},{11,1... | collective-permute-start | bytes 3128 | tf_op jit(solution)/shard_map/while/body/eval_jaxpr/ppermute | solution.py:39
  98.2 6.3 %collective-permute-start.3 = (f32[2,130,1]{2,1,0:T(8,128)}, f32[2,130,1]{2,1,0:T(8,128)}, u32[]{:S(2)}, u32[]{:S(2)}) collective-permute-start(f32[2,130,1]{2,1,0:T(8,128)} %get-tuple-element.620), channel_id=1, source_target_pairs={{0,1},{1,2},{2,3},{3,0},{4,5},{5,6},{6,7},{7,4},{8,9},{9,10},{10,1... | collective-permute-start | bytes 3128 | tf_op jit(solution)/shard_map/while/body/eval_jaxpr/ppermute | solution.py:38
  109.4 1.4 collective-permute-start
  109.4 4.9 %collective-permute-start.1 = (f32[2,1,512]{2,1,0:T(1,128)S(1)}, f32[2,1,512]{2,1,0:T(1,128)S(1)}, u32[]{:S(2)}, u32[]{:S(2)}) collective-permute-start(f32[2,1,512]{2,1,0:T(1,128)S(1)} %get-tuple-element.618), channel_id=1, source_target_pairs={{0,4},{4,8},{8,12},{12,16},{16,20},{20,24},{24,28},{28,0},{1,5},{5... | collective-permute-start | bytes 12296 | tf_op jit(solution)/shard_map/while/body/eval_jaxpr/ppermute | solution.py:38
  115.1 5.3 %collective-permute-start.2 = (f32[2,130,1]{2,1,0:T(8,128)}, f32[2,130,1]{2,1,0:T(8,128)S(1)}, u32[]{:S(2)}, u32[]{:S(2)}) collective-permute-start(f32[2,130,1]{2,1,0:T(8,128)} %get-tuple-element.619), channel_id=1, source_target_pairs={{1,0},{2,1},{3,2},{0,3},{5,4},{6,5},{7,6},{4,7},{9,8},{10,9},{11,1... | collective-permute-start | bytes 3128 | tf_op jit(solution)/shard_map/while/body/eval_jaxpr/ppermute | solution.py:39
  116.8 6.3 %collective-permute-start.3 = (f32[2,130,1]{2,1,0:T(8,128)}, f32[2,130,1]{2,1,0:T(8,128)}, u32[]{:S(2)}, u32[]{:S(2)}) collective-permute-start(f32[2,130,1]{2,1,0:T(8,128)} %get-tuple-element.620), channel_id=1, source_target_pairs={{0,1},{1,2},{2,3},{3,0},{4,5},{5,6},{6,7},{7,4},{8,9},{9,10},{10,1... | collective-permute-start | bytes 3128 | tf_op jit(solution)/shard_map/while/body/eval_jaxpr/ppermute | solution.py:38
  128.0 1.4 collective-permute-start
  128.1 4.9 %collective-permute-start.1 = (f32[2,1,512]{2,1,0:T(1,128)S(1)}, f32[2,1,512]{2,1,0:T(1,128)S(1)}, u32[]{:S(2)}, u32[]{:S(2)}) collective-permute-start(f32[2,1,512]{2,1,0:T(1,128)S(1)} %get-tuple-element.618), channel_id=1, source_target_pairs={{0,4},{4,8},{8,12},{12,16},{16,20},{20,24},{24,28},{28,0},{1,5},{5... | collective-permute-start | bytes 12296 | tf_op jit(solution)/shard_map/while/body/eval_jaxpr/ppermute | solution.py:38
  133.8 5.3 %collective-permute-start.2 = (f32[2,130,1]{2,1,0:T(8,128)}, f32[2,130,1]{2,1,0:T(8,128)S(1)}, u32[]{:S(2)}, u32[]{:S(2)}) collective-permute-start(f32[2,130,1]{2,1,0:T(8,128)} %get-tuple-element.619), channel_id=1, source_target_pairs={{1,0},{2,1},{3,2},{0,3},{5,4},{6,5},{7,6},{4,7},{9,8},{10,9},{11,1... | collective-permute-start | bytes 3128 | tf_op jit(solution)/shard_map/while/body/eval_jaxpr/ppermute | solution.py:39
  134.3 6.3 %collective-permute-start.3 = (f32[2,130,1]{2,1,0:T(8,128)}, f32[2,130,1]{2,1,0:T(8,128)}, u32[]{:S(2)}, u32[]{:S(2)}) collective-permute-start(f32[2,130,1]{2,1,0:T(8,128)} %get-tuple-element.620), channel_id=1, source_target_pairs={{0,1},{1,2},{2,3},{3,0},{4,5},{5,6},{6,7},{7,4},{8,9},{9,10},{10,1... | collective-permute-start | bytes 3128 | tf_op jit(solution)/shard_map/while/body/eval_jaxpr/ppermute | solution.py:38
  145.5 1.4 collective-permute-start
  145.6 4.9 %collective-permute-start.1 = (f32[2,1,512]{2,1,0:T(1,128)S(1)}, f32[2,1,512]{2,1,0:T(1,128)S(1)}, u32[]{:S(2)}, u32[]{:S(2)}) collective-permute-start(f32[2,1,512]{2,1,0:T(1,128)S(1)} %get-tuple-element.618), channel_id=1, source_target_pairs={{0,4},{4,8},{8,12},{12,16},{16,20},{20,24},{24,28},{28,0},{1,5},{5... | collective-permute-start | bytes 12296 | tf_op jit(solution)/shard_map/while/body/eval_jaxpr/ppermute | solution.py:38
  151.2 5.3 %collective-permute-start.2 = (f32[2,130,1]{2,1,0:T(8,128)}, f32[2,130,1]{2,1,0:T(8,128)S(1)}, u32[]{:S(2)}, u32[]{:S(2)}) collective-permute-start(f32[2,130,1]{2,1,0:T(8,128)} %get-tuple-element.619), channel_id=1, source_target_pairs={{1,0},{2,1},{3,2},{0,3},{5,4},{6,5},{7,6},{4,7},{9,8},{10,9},{11,1... | collective-permute-start | bytes 3128 | tf_op jit(solution)/shard_map/while/body/eval_jaxpr/ppermute | solution.py:39
  152.8 6.3 %collective-permute-start.3 = (f32[2,130,1]{2,1,0:T(8,128)}, f32[2,130,1]{2,1,0:T(8,128)}, u32[]{:S(2)}, u32[]{:S(2)}) collective-permute-start(f32[2,130,1]{2,1,0:T(8,128)} %get-tuple-element.620), channel_id=1, source_target_pairs={{0,1},{1,2},{2,3},{3,0},{4,5},{5,6},{6,7},{7,4},{8,9},{9,10},{10,1... | collective-permute-start | bytes 3128 | tf_op jit(solution)/shard_map/while/body/eval_jaxpr/ppermute | solution.py:38
  164.0 4.9 %collective-permute-start.1 = (f32[2,1,512]{2,1,0:T(1,128)S(1)}, f32[2,1,512]{2,1,0:T(1,128)S(1)}, u32[]{:S(2)}, u32[]{:S(2)}) collective-permute-start(f32[2,1,512]{2,1,0:T(1,128)S(1)} %get-tuple-element.618), channel_id=1, source_target_pairs={{0,4},{4,8},{8,12},{12,16},{16,20},{20,24},{24,28},{28,0},{1,5},{5... | collective-permute-start | bytes 12296 | tf_op jit(solution)/shard_map/while/body/eval_jaxpr/ppermute | solution.py:38
  169.7 5.3 %collective-permute-start.2 = (f32[2,130,1]{2,1,0:T(8,128)}, f32[2,130,1]{2,1,0:T(8,128)S(1)}, u32[]{:S(2)}, u32[]{:S(2)}) collective-permute-start(f32[2,130,1]{2,1,0:T(8,128)} %get-tuple-element.619), channel_id=1, source_target_pairs={{1,0},{2,1},{3,2},{0,3},{5,4},{6,5},{7,6},{4,7},{9,8},{10,9},{11,1... | collective-permute-start | bytes 3128 | tf_op jit(solution)/shard_map/while/body/eval_jaxpr/ppermute | solution.py:39
  170.2 6.3 %collective-permute-start.3 = (f32[2,130,1]{2,1,0:T(8,128)}, f32[2,130,1]{2,1,0:T(8,128)}, u32[]{:S(2)}, u32[]{:S(2)}) collective-permute-start(f32[2,130,1]{2,1,0:T(8,128)} %get-tuple-element.620), channel_id=1, source_target_pairs={{0,1},{1,2},{2,3},{3,0},{4,5},{5,6},{6,7},{7,4},{8,9},{9,10},{10,1... | collective-permute-start | bytes 3128 | tf_op jit(solution)/shard_map/while/body/eval_jaxpr/ppermute | solution.py:38
  181.5 4.9 %collective-permute-start.1 = (f32[2,1,512]{2,1,0:T(1,128)S(1)}, f32[2,1,512]{2,1,0:T(1,128)S(1)}, u32[]{:S(2)}, u32[]{:S(2)}) collective-permute-start(f32[2,1,512]{2,1,0:T(1,128)S(1)} %get-tuple-element.618), channel_id=1, source_target_pairs={{0,4},{4,8},{8,12},{12,16},{16,20},{20,24},{24,28},{28,0},{1,5},{5... | collective-permute-start | bytes 12296 | tf_op jit(solution)/shard_map/while/body/eval_jaxpr/ppermute | solution.py:38
  187.2 5.3 %collective-permute-start.2 = (f32[2,130,1]{2,1,0:T(8,128)}, f32[2,130,1]{2,1,0:T(8,128)S(1)}, u32[]{:S(2)}, u32[]{:S(2)}) collective-permute-start(f32[2,130,1]{2,1,0:T(8,128)} %get-tuple-element.619), channel_id=1, source_target_pairs={{1,0},{2,1},{3,2},{0,3},{5,4},{6,5},{7,6},{4,7},{9,8},{10,9},{11,1... | collective-permute-start | bytes 3128 | tf_op jit(solution)/shard_map/while/body/eval_jaxpr/ppermute | solution.py:39
  188.7 6.3 %collective-permute-start.3 = (f32[2,130,1]{2,1,0:T(8,128)}, f32[2,130,1]{2,1,0:T(8,128)}, u32[]{:S(2)}, u32[]{:S(2)}) collective-permute-start(f32[2,130,1]{2,1,0:T(8,128)} %get-tuple-element.620), channel_id=1, source_target_pairs={{0,1},{1,2},{2,3},{3,0},{4,5},{5,6},{6,7},{7,4},{8,9},{9,10},{10,1... | collective-permute-start | bytes 3128 | tf_op jit(solution)/shard_map/while/body/eval_jaxpr/ppermute | solution.py:38
  200.0 4.9 %collective-permute-start.1 = (f32[2,1,512]{2,1,0:T(1,128)S(1)}, f32[2,1,512]{2,1,0:T(1,128)S(1)}, u32[]{:S(2)}, u32[]{:S(2)}) collective-permute-start(f32[2,1,512]{2,1,0:T(1,128)S(1)} %get-tuple-element.618), channel_id=1, source_target_pairs={{0,4},{4,8},{8,12},{12,16},{16,20},{20,24},{24,28},{28,0},{1,5},{5... | collective-permute-start | bytes 12296 | tf_op jit(solution)/shard_map/while/body/eval_jaxpr/ppermute | solution.py:38
  205.6 5.3 %collective-permute-start.2 = (f32[2,130,1]{2,1,0:T(8,128)}, f32[2,130,1]{2,1,0:T(8,128)S(1)}, u32[]{:S(2)}, u32[]{:S(2)}) collective-permute-start(f32[2,130,1]{2,1,0:T(8,128)} %get-tuple-element.619), channel_id=1, source_target_pairs={{1,0},{2,1},{3,2},{0,3},{5,4},{6,5},{7,6},{4,7},{9,8},{10,9},{11,1... | collective-permute-start | bytes 3128 | tf_op jit(solution)/shard_map/while/body/eval_jaxpr/ppermute | solution.py:39
  206.2 6.3 %collective-permute-start.3 = (f32[2,130,1]{2,1,0:T(8,128)}, f32[2,130,1]{2,1,0:T(8,128)}, u32[]{:S(2)}, u32[]{:S(2)}) collective-permute-start(f32[2,130,1]{2,1,0:T(8,128)} %get-tuple-element.620), channel_id=1, source_target_pairs={{0,1},{1,2},{2,3},{3,0},{4,5},{5,6},{6,7},{7,4},{8,9},{9,10},{10,1... | collective-permute-start | bytes 3128 | tf_op jit(solution)/shard_map/while/body/eval_jaxpr/ppermute | solution.py:38
  217.4 4.9 %collective-permute-start.1 = (f32[2,1,512]{2,1,0:T(1,128)S(1)}, f32[2,1,512]{2,1,0:T(1,128)S(1)}, u32[]{:S(2)}, u32[]{:S(2)}) collective-permute-start(f32[2,1,512]{2,1,0:T(1,128)S(1)} %get-tuple-element.618), channel_id=1, source_target_pairs={{0,4},{4,8},{8,12},{12,16},{16,20},{20,24},{24,28},{28,0},{1,5},{5... | collective-permute-start | bytes 12296 | tf_op jit(solution)/shard_map/while/body/eval_jaxpr/ppermute | solution.py:38
  223.1 5.3 %collective-permute-start.2 = (f32[2,130,1]{2,1,0:T(8,128)}, f32[2,130,1]{2,1,0:T(8,128)S(1)}, u32[]{:S(2)}, u32[]{:S(2)}) collective-permute-start(f32[2,130,1]{2,1,0:T(8,128)} %get-tuple-element.619), channel_id=1, source_target_pairs={{1,0},{2,1},{3,2},{0,3},{5,4},{6,5},{7,6},{4,7},{9,8},{10,9},{11,1... | collective-permute-start | bytes 3128 | tf_op jit(solution)/shard_map/while/body/eval_jaxpr/ppermute | solution.py:39
  224.6 6.3 %collective-permute-start.3 = (f32[2,130,1]{2,1,0:T(8,128)}, f32[2,130,1]{2,1,0:T(8,128)}, u32[]{:S(2)}, u32[]{:S(2)}) collective-permute-start(f32[2,130,1]{2,1,0:T(8,128)} %get-tuple-element.620), channel_id=1, source_target_pairs={{0,1},{1,2},{2,3},{3,0},{4,5},{5,6},{6,7},{7,4},{8,9},{9,10},{10,1... | collective-permute-start | bytes 3128 | tf_op jit(solution)/shard_map/while/body/eval_jaxpr/ppermute | solution.py:38
  235.9 4.9 %collective-permute-start.1 = (f32[2,1,512]{2,1,0:T(1,128)S(1)}, f32[2,1,512]{2,1,0:T(1,128)S(1)}, u32[]{:S(2)}, u32[]{:S(2)}) collective-permute-start(f32[2,1,512]{2,1,0:T(1,128)S(1)} %get-tuple-element.618), channel_id=1, source_target_pairs={{0,4},{4,8},{8,12},{12,16},{16,20},{20,24},{24,28},{28,0},{1,5},{5... | collective-permute-start | bytes 12296 | tf_op jit(solution)/shard_map/while/body/eval_jaxpr/ppermute | solution.py:38
  241.6 5.3 %collective-permute-start.2 = (f32[2,130,1]{2,1,0:T(8,128)}, f32[2,130,1]{2,1,0:T(8,128)S(1)}, u32[]{:S(2)}, u32[]{:S(2)}) collective-permute-start(f32[2,130,1]{2,1,0:T(8,128)} %get-tuple-element.619), channel_id=1, source_target_pairs={{1,0},{2,1},{3,2},{0,3},{5,4},{6,5},{7,6},{4,7},{9,8},{10,9},{11,1... | collective-permute-start | bytes 3128 | tf_op jit(solution)/shard_map/while/body/eval_jaxpr/ppermute | solution.py:39
  242.1 6.3 %collective-permute-start.3 = (f32[2,130,1]{2,1,0:T(8,128)}, f32[2,130,1]{2,1,0:T(8,128)}, u32[]{:S(2)}, u32[]{:S(2)}) collective-permute-start(f32[2,130,1]{2,1,0:T(8,128)} %get-tuple-element.620), channel_id=1, source_target_pairs={{0,1},{1,2},{2,3},{3,0},{4,5},{5,6},{6,7},{7,4},{8,9},{9,10},{10,1... | collective-permute-start | bytes 3128 | tf_op jit(solution)/shard_map/while/body/eval_jaxpr/ppermute | solution.py:38
  253.4 4.9 %collective-permute-start.1 = (f32[2,1,512]{2,1,0:T(1,128)S(1)}, f32[2,1,512]{2,1,0:T(1,128)S(1)}, u32[]{:S(2)}, u32[]{:S(2)}) collective-permute-start(f32[2,1,512]{2,1,0:T(1,128)S(1)} %get-tuple-element.618), channel_id=1, source_target_pairs={{0,4},{4,8},{8,12},{12,16},{16,20},{20,24},{24,28},{28,0},{1,5},{5... | collective-permute-start | bytes 12296 | tf_op jit(solution)/shard_map/while/body/eval_jaxpr/ppermute | solution.py:38
  259.0 5.3 %collective-permute-start.2 = (f32[2,130,1]{2,1,0:T(8,128)}, f32[2,130,1]{2,1,0:T(8,128)S(1)}, u32[]{:S(2)}, u32[]{:S(2)}) collective-permute-start(f32[2,130,1]{2,1,0:T(8,128)} %get-tuple-element.619), channel_id=1, source_target_pairs={{1,0},{2,1},{3,2},{0,3},{5,4},{6,5},{7,6},{4,7},{9,8},{10,9},{11,1... | collective-permute-start | bytes 3128 | tf_op jit(solution)/shard_map/while/body/eval_jaxpr/ppermute | solution.py:39
  260.6 6.3 %collective-permute-start.3 = (f32[2,130,1]{2,1,0:T(8,128)}, f32[2,130,1]{2,1,0:T(8,128)}, u32[]{:S(2)}, u32[]{:S(2)}) collective-permute-start(f32[2,130,1]{2,1,0:T(8,128)} %get-tuple-element.620), channel_id=1, source_target_pairs={{0,1},{1,2},{2,3},{3,0},{4,5},{5,6},{6,7},{7,4},{8,9},{9,10},{10,1... | collective-permute-start | bytes 3128 | tf_op jit(solution)/shard_map/while/body/eval_jaxpr/ppermute | solution.py:38
  271.8 4.9 %collective-permute-start.1 = (f32[2,1,512]{2,1,0:T(1,128)S(1)}, f32[2,1,512]{2,1,0:T(1,128)S(1)}, u32[]{:S(2)}, u32[]{:S(2)}) collective-permute-start(f32[2,1,512]{2,1,0:T(1,128)S(1)} %get-tuple-element.618), channel_id=1, source_target_pairs={{0,4},{4,8},{8,12},{12,16},{16,20},{20,24},{24,28},{28,0},{1,5},{5... | collective-permute-start | bytes 12296 | tf_op jit(solution)/shard_map/while/body/eval_jaxpr/ppermute | solution.py:38
  277.5 5.3 %collective-permute-start.2 = (f32[2,130,1]{2,1,0:T(8,128)}, f32[2,130,1]{2,1,0:T(8,128)S(1)}, u32[]{:S(2)}, u32[]{:S(2)}) collective-permute-start(f32[2,130,1]{2,1,0:T(8,128)} %get-tuple-element.619), channel_id=1, source_target_pairs={{1,0},{2,1},{3,2},{0,3},{5,4},{6,5},{7,6},{4,7},{9,8},{10,9},{11,1... | collective-permute-start | bytes 3128 | tf_op jit(solution)/shard_map/while/body/eval_jaxpr/ppermute | solution.py:39
  278.0 6.3 %collective-permute-start.3 = (f32[2,130,1]{2,1,0:T(8,128)}, f32[2,130,1]{2,1,0:T(8,128)}, u32[]{:S(2)}, u32[]{:S(2)}) collective-permute-start(f32[2,130,1]{2,1,0:T(8,128)} %get-tuple-element.620), channel_id=1, source_target_pairs={{0,1},{1,2},{2,3},{3,0},{4,5},{5,6},{6,7},{7,4},{8,9},{9,10},{10,1... | collective-permute-start | bytes 3128 | tf_op jit(solution)/shard_map/while/body/eval_jaxpr/ppermute | solution.py:38
  289.3 4.9 %collective-permute-start.1 = (f32[2,1,512]{2,1,0:T(1,128)S(1)}, f32[2,1,512]{2,1,0:T(1,128)S(1)}, u32[]{:S(2)}, u32[]{:S(2)}) collective-permute-start(f32[2,1,512]{2,1,0:T(1,128)S(1)} %get-tuple-element.618), channel_id=1, source_target_pairs={{0,4},{4,8},{8,12},{12,16},{16,20},{20,24},{24,28},{28,0},{1,5},{5... | collective-permute-start | bytes 12296 | tf_op jit(solution)/shard_map/while/body/eval_jaxpr/ppermute | solution.py:38
  295.0 5.3 %collective-permute-start.2 = (f32[2,130,1]{2,1,0:T(8,128)}, f32[2,130,1]{2,1,0:T(8,128)S(1)}, u32[]{:S(2)}, u32[]{:S(2)}) collective-permute-start(f32[2,130,1]{2,1,0:T(8,128)} %get-tuple-element.619), channel_id=1, source_target_pairs={{1,0},{2,1},{3,2},{0,3},{5,4},{6,5},{7,6},{4,7},{9,8},{10,9},{11,1... | collective-permute-start | bytes 3128 | tf_op jit(solution)/shard_map/while/body/eval_jaxpr/ppermute | solution.py:39
  296.5 6.3 %collective-permute-start.3 = (f32[2,130,1]{2,1,0:T(8,128)}, f32[2,130,1]{2,1,0:T(8,128)}, u32[]{:S(2)}, u32[]{:S(2)}) collective-permute-start(f32[2,130,1]{2,1,0:T(8,128)} %get-tuple-element.620), channel_id=1, source_target_pairs={{0,1},{1,2},{2,3},{3,0},{4,5},{5,6},{6,7},{7,4},{8,9},{9,10},{10,1... | collective-permute-start | bytes 3128 | tf_op jit(solution)/shard_map/while/body/eval_jaxpr/ppermute | solution.py:38
  307.8 4.9 %collective-permute-start.1 = (f32[2,1,512]{2,1,0:T(1,128)S(1)}, f32[2,1,512]{2,1,0:T(1,128)S(1)}, u32[]{:S(2)}, u32[]{:S(2)}) collective-permute-start(f32[2,1,512]{2,1,0:T(1,128)S(1)} %get-tuple-element.618), channel_id=1, source_target_pairs={{0,4},{4,8},{8,12},{12,16},{16,20},{20,24},{24,28},{28,0},{1,5},{5... | collective-permute-start | bytes 12296 | tf_op jit(solution)/shard_map/while/body/eval_jaxpr/ppermute | solution.py:38
  313.4 5.3 %collective-permute-start.2 = (f32[2,130,1]{2,1,0:T(8,128)}, f32[2,130,1]{2,1,0:T(8,128)S(1)}, u32[]{:S(2)}, u32[]{:S(2)}) collective-permute-start(f32[2,130,1]{2,1,0:T(8,128)} %get-tuple-element.619), channel_id=1, source_target_pairs={{1,0},{2,1},{3,2},{0,3},{5,4},{6,5},{7,6},{4,7},{9,8},{10,9},{11,1... | collective-permute-start | bytes 3128 | tf_op jit(solution)/shard_map/while/body/eval_jaxpr/ppermute | solution.py:39
  314.0 6.3 %collective-permute-start.3 = (f32[2,130,1]{2,1,0:T(8,128)}, f32[2,130,1]{2,1,0:T(8,128)}, u32[]{:S(2)}, u32[]{:S(2)}) collective-permute-start(f32[2,130,1]{2,1,0:T(8,128)} %get-tuple-element.620), channel_id=1, source_target_pairs={{0,1},{1,2},{2,3},{3,0},{4,5},{5,6},{6,7},{7,4},{8,9},{9,10},{10,1... | collective-permute-start | bytes 3128 | tf_op jit(solution)/shard_map/while/body/eval_jaxpr/ppermute | solution.py:38
  325.2 4.9 %collective-permute-start.1 = (f32[2,1,512]{2,1,0:T(1,128)S(1)}, f32[2,1,512]{2,1,0:T(1,128)S(1)}, u32[]{:S(2)}, u32[]{:S(2)}) collective-permute-start(f32[2,1,512]{2,1,0:T(1,128)S(1)} %get-tuple-element.618), channel_id=1, source_target_pairs={{0,4},{4,8},{8,12},{12,16},{16,20},{20,24},{24,28},{28,0},{1,5},{5... | collective-permute-start | bytes 12296 | tf_op jit(solution)/shard_map/while/body/eval_jaxpr/ppermute | solution.py:38
  330.9 5.3 %collective-permute-start.2 = (f32[2,130,1]{2,1,0:T(8,128)}, f32[2,130,1]{2,1,0:T(8,128)S(1)}, u32[]{:S(2)}, u32[]{:S(2)}) collective-permute-start(f32[2,130,1]{2,1,0:T(8,128)} %get-tuple-element.619), channel_id=1, source_target_pairs={{1,0},{2,1},{3,2},{0,3},{5,4},{6,5},{7,6},{4,7},{9,8},{10,9},{11,1... | collective-permute-start | bytes 3128 | tf_op jit(solution)/shard_map/while/body/eval_jaxpr/ppermute | solution.py:39
  332.4 6.3 %collective-permute-start.3 = (f32[2,130,1]{2,1,0:T(8,128)}, f32[2,130,1]{2,1,0:T(8,128)}, u32[]{:S(2)}, u32[]{:S(2)}) collective-permute-start(f32[2,130,1]{2,1,0:T(8,128)} %get-tuple-element.620), channel_id=1, source_target_pairs={{0,1},{1,2},{2,3},{3,0},{4,5},{5,6},{6,7},{7,4},{8,9},{9,10},{10,1... | collective-permute-start | bytes 3128 | tf_op jit(solution)/shard_map/while/body/eval_jaxpr/ppermute | solution.py:38
  343.6 1.4 collective-permute-start
  343.7 4.9 %collective-permute-start.1 = (f32[2,1,512]{2,1,0:T(1,128)S(1)}, f32[2,1,512]{2,1,0:T(1,128)S(1)}, u32[]{:S(2)}, u32[]{:S(2)}) collective-permute-start(f32[2,1,512]{2,1,0:T(1,128)S(1)} %get-tuple-element.618), channel_id=1, source_target_pairs={{0,4},{4,8},{8,12},{12,16},{16,20},{20,24},{24,28},{28,0},{1,5},{5... | collective-permute-start | bytes 12296 | tf_op jit(solution)/shard_map/while/body/eval_jaxpr/ppermute | solution.py:38
  349.4 5.3 %collective-permute-start.2 = (f32[2,130,1]{2,1,0:T(8,128)}, f32[2,130,1]{2,1,0:T(8,128)S(1)}, u32[]{:S(2)}, u32[]{:S(2)}) collective-permute-start(f32[2,130,1]{2,1,0:T(8,128)} %get-tuple-element.619), channel_id=1, source_target_pairs={{1,0},{2,1},{3,2},{0,3},{5,4},{6,5},{7,6},{4,7},{9,8},{10,9},{11,1... | collective-permute-start | bytes 3128 | tf_op jit(solution)/shard_map/while/body/eval_jaxpr/ppermute | solution.py:39
  349.9 6.3 %collective-permute-start.3 = (f32[2,130,1]{2,1,0:T(8,128)}, f32[2,130,1]{2,1,0:T(8,128)}, u32[]{:S(2)}, u32[]{:S(2)}) collective-permute-start(f32[2,130,1]{2,1,0:T(8,128)} %get-tuple-element.620), channel_id=1, source_target_pairs={{0,1},{1,2},{2,3},{3,0},{4,5},{5,6},{6,7},{7,4},{8,9},{9,10},{10,1... | collective-permute-start | bytes 3128 | tf_op jit(solution)/shard_map/while/body/eval_jaxpr/ppermute | solution.py:38
  361.1 4.9 %collective-permute-start.1 = (f32[2,1,512]{2,1,0:T(1,128)S(1)}, f32[2,1,512]{2,1,0:T(1,128)S(1)}, u32[]{:S(2)}, u32[]{:S(2)}) collective-permute-start(f32[2,1,512]{2,1,0:T(1,128)S(1)} %get-tuple-element.618), channel_id=1, source_target_pairs={{0,4},{4,8},{8,12},{12,16},{16,20},{20,24},{24,28},{28,0},{1,5},{5... | collective-permute-start | bytes 12296 | tf_op jit(solution)/shard_map/while/body/eval_jaxpr/ppermute | solution.py:38
  366.8 5.3 %collective-permute-start.2 = (f32[2,130,1]{2,1,0:T(8,128)}, f32[2,130,1]{2,1,0:T(8,128)S(1)}, u32[]{:S(2)}, u32[]{:S(2)}) collective-permute-start(f32[2,130,1]{2,1,0:T(8,128)} %get-tuple-element.619), channel_id=1, source_target_pairs={{1,0},{2,1},{3,2},{0,3},{5,4},{6,5},{7,6},{4,7},{9,8},{10,9},{11,1... | collective-permute-start | bytes 3128 | tf_op jit(solution)/shard_map/while/body/eval_jaxpr/ppermute | solution.py:39
  368.4 6.3 %collective-permute-start.3 = (f32[2,130,1]{2,1,0:T(8,128)}, f32[2,130,1]{2,1,0:T(8,128)}, u32[]{:S(2)}, u32[]{:S(2)}) collective-permute-start(f32[2,130,1]{2,1,0:T(8,128)} %get-tuple-element.620), channel_id=1, source_target_pairs={{0,1},{1,2},{2,3},{3,0},{4,5},{5,6},{6,7},{7,4},{8,9},{9,10},{10,1... | collective-permute-start | bytes 3128 | tf_op jit(solution)/shard_map/while/body/eval_jaxpr/ppermute | solution.py:38
  380.5 4.9 %collective-permute-start.11 = (f32[4,1,512]{2,1,0:T(1,128)S(1)}, f32[4,1,512]{2,1,0:T(1,128)S(1)}, u32[]{:S(2)}, u32[]{:S(2)}) collective-permute-start(f32[4,1,512]{2,1,0:T(1,128)S(1)} %get-tuple-element.512), channel_id=1, source_target_pairs={{0,4},{4,8},{8,12},{12,16},{16,20},{20,24},{24,28},{28,0},{1,5},{5... | collective-permute-start | bytes 24584 | tf_op jit(solution)/shard_map/ppermute | solution.py:38
  380.5 4.9 %collective-permute-start.12 = (f32[4,1,512]{2,1,0:T(1,128)S(1)}, f32[4,1,512]{2,1,0:T(1,128)S(1)}, u32[]{:S(2)}, u32[]{:S(2)}) collective-permute-start(f32[4,1,512]{2,1,0:T(1,128)S(1)} %get-tuple-element.513), channel_id=1, source_target_pairs={{4,0},{8,4},{12,8},{16,12},{20,16},{24,20},{28,24},{0,28},{5,1},{9... | collective-permute-start | bytes 24584 | tf_op jit(solution)/shard_map/ppermute | solution.py:39
  386.6 9.3 %collective-permute-start.13 = (f32[4,130,1]{2,1,0:T(8,128)S(1)}, f32[4,130,1]{2,1,0:T(8,128)S(1)}, u32[]{:S(2)}, u32[]{:S(2)}) collective-permute-start(f32[4,130,1]{2,1,0:T(8,128)S(1)} %get-tuple-element.510), channel_id=1, source_target_pairs={{0,1},{1,2},{2,3},{3,0},{4,5},{5,6},{6,7},{7,4},{8,9},{9,10},{10,1... | collective-permute-start | bytes 6248 | tf_op jit(solution)/shard_map/ppermute | solution.py:38
  387.3 10.7 %collective-permute-start.14 = (f32[4,130,1]{2,1,0:T(8,128)S(1)}, f32[4,130,1]{2,1,0:T(8,128)S(1)}, u32[]{:S(2)}, u32[]{:S(2)}) collective-permute-start(f32[4,130,1]{2,1,0:T(8,128)S(1)} %get-tuple-element.511), channel_id=1, source_target_pairs={{1,0},{2,1},{3,2},{0,3},{5,4},{6,5},{7,6},{4,7},{9,8},{10,9},{11,1... | collective-permute-start | bytes 6248 | tf_op jit(solution)/shard_map/ppermute | solution.py:39
  (31 other events, 155.8 us)
where the time goes:
time: 443 us; the launch traced here: 442 us
  waiting for transfers between devices  209 us (47%)
  other arithmetic  105 us (24%)
  starting transfers between devices  62.4 us (14%)
  blocking collectives  38.6 us (9%)
  local copies, waits for them, and re-layouts  24.3 us (5%)
    ppermute x36, waiting for transfers between devices, padded(): before = lax.ppermute(last, axis, up)  103 us
    ppermute x3, waiting for transfers between devices, swapped(): lax.ppermute(array, axis, [(i, i ^ 1 << bit) for i in range(lax.axis_size...  53.8 us
    ppermute x36, waiting for transfers between devices, padded(): after = lax.ppermute(initial, axis, down)  52.1 us
    pmax x1, blocking collectives, shards(): lax.pmax(jnp.max(jnp.abs(drift_east) + jnp.abs(drift_north)), ('lat', 'lo...  38.6 us
    ppermute x36, starting transfers between devices, padded(): after = lax.ppermute(initial, axis, down)  33.3 us
    add x16, other arithmetic, group(): first_table[position] * update_ext + second_table[position] * scaled  27.9 us
    sub x16, other arithmetic, apply_operator(): result - weights[index_pair] * window(field_ext, shift_lat, shift_lon)  26.5 us
    ppermute x36, starting transfers between devices, padded(): before = lax.ppermute(last, axis, up)  22.9 us
  transfers between devices with their start and end apart: 75, of which 73 were waited for; matrix products, arithmetic and copies ran while one was open for 5% of the time, Pallas kernels for 0%

commit v1 on v0

v1 whole, which is shorter than its diff:
```python
import functools

import jax
import jax.numpy as jnp
from jax import lax
from jax.experimental import pallas as pl
from jax.experimental.pallas import tpu as pltpu
from jax.sharding import PartitionSpec as P

SWEEPS = 16
DAMPING = 0.0001
LOW_BOUND = 0.05
HIGH_BOUND = 2.0
COURANT = 0.8
MOBILITY = (1.0, 0.6, 0.3)
MESH = pl.DeviceIdType.MESH
HALO = 24
F32 = jnp.float32


def chebyshev_factors():
    theta = 0.5 * (HIGH_BOUND + LOW_BOUND)
    delta = 0.5 * (HIGH_BOUND - LOW_BOUND)
    sigma_one = theta / delta
    rho_prev = 1.0 / sigma_one
    first_list = []
    second_list = []
    for sweep in range(SWEEPS):
        rho_next = 1.0 / (2.0 * sigma_one - rho_prev)
        first_list.append(rho_next * rho_prev)
        second_list.append(2.0 * rho_next / delta)
        rho_prev = rho_next
    return (theta, first_list, second_list)


def kernel(
    nlat, nlon, lev, rows, lt,
    coef, ped_h, hall_h, east_h, north_h, ion_h,
    pot_h, upd_h,
    ped, hall, east, north,
    ion, ion_fr, ion_fl,
    sig, cur_e, cur_n, e_fr, e_fl, s_one, t_out, sig_rx, t_rx,
    S, src, pk_l, pk_r, rx_fr, rx_fl,
    g, r, sp, x, d, u, w,
    flux, upd, mx, rx_lat, mx2, rx_lon,
    sem_in, sem_ion, sem_out, ss, rs, ss_lat, rs_lat, ss_lon, rs_lon,
):
    n_rt = rows // 8
    nt = lt + 1
    me_lat = lax.axis_index("lat")
    me_lon = lax.axis_index("lon")
    has_up = me_lat > 0
    has_dn = me_lat < nlat - 1
    up = (jnp.maximum(me_lat - 1, 0), me_lon)
    dn = (jnp.minimum(me_lat + 1, nlat - 1), me_lon)
    lf = (me_lat, lax.rem(me_lon + nlon - 1, nlon))
    rt = (me_lat, lax.rem(me_lon + 1, nlon))
    mirror = (nlat - 1 - me_lat, me_lon)

    order = [0, n_rt - 1] + list(range(1, n_rt - 1))
    hbm_in = (ped_h, hall_h, east_h, north_h)
    vm_in = (ped, hall, east, north)

    def in_copy(a, row, slot):
        return pltpu.make_async_copy(
            hbm_in[a].at[:, pl.ds(row, 8), :], vm_in[a].at[:, pl.ds(row, 8), :], sem_in.at[slot, a]
        )

    def ion_copy(s, t):
        return pltpu.make_async_copy(
            ion_h.at[s, :, t * 128 : (t + 1) * 128], ion.at[s, t, 8 : 8 + rows], sem_ion.at[s, t]
        )

    for c in order[:2]:
        for a in range(4):
            in_copy(a, 8 * c, c).start()
    for s in range(3):
        for t in range(lt):
            ion_copy(s, t).start()
    for c in order[2:]:
        for a in range(4):
            in_copy(a, 8 * c, c).start()

    barrier = pltpu.get_barrier_semaphore()
    for o in range(1, nlat):
        pl.semaphore_signal(
            barrier, inc=1, device_id=(lax.rem(me_lat + o, nlat), me_lon), device_id_type=MESH
        )
    for o in range(1, nlon):
        pl.semaphore_signal(
            barrier, inc=1, device_id=(me_lat, lax.rem(me_lon + o, nlon)), device_id_type=MESH
        )
    pl.semaphore_wait(barrier, nlat + nlon - 2)

    def rcopy(src_ref, dst_ref, k, dev):
        return pltpu.make_async_remote_copy(
            src_ref=src_ref, dst_ref=dst_ref, send_sem=ss.at[k], recv_sem=rs.at[k],
            device_id=dev, device_id_type=MESH,
        )

    lane = lax.broadcasted_iota(jnp.int32, (8, 128), 1)
    sub = lax.broadcasted_iota(jnp.int32, (8, 128), 0)

    def shifts(v):
        m = len(v)
        a = [pltpu.roll(t, 1, 1) for t in v]
        b = [pltpu.roll(t, 127, 1) for t in v]
        left = [jnp.where(lane == 0, a[j - 1], a[j]) for j in range(m)]
        right = [jnp.where(lane == 127, b[(j + 1) % m], b[j]) for j in range(m)]
        return left, right

    def smooth(v):
        left, right = shifts(v)
        return [t + 0.5 * (p + q) for t, p, q in zip(v, left, right)]

    def rev8(v):
        v = pltpu.roll(v, 4, 0)
        for b in (2, 1):
            v = jnp.where((sub & b) == 0, pltpu.roll(v, 8 - b, 0), pltpu.roll(v, b, 0))
        return v

    weight = [(0.5 + l / lev) / lev for l in range(lev)]

    def columns(c):
        row = pl.multiple_of(8 * c, 8)
        for a in range(4):
            in_copy(a, row, c).wait()
        for t in range(lt):
            at = (pl.ds(row, 8), slice(t * 128, (t + 1) * 128))
            acc = [jnp.zeros((8, 128), F32)] * 3
            for l in range(lev):
                p, h = weight[l] * ped[(l,) + at], weight[l] * hall[(l,) + at]
                e, n = east[(l,) + at], north[(l,) + at]
                acc = [acc[0] + p, acc[1] + (p * e + h * n), acc[2] + (p * n - h * e)]
            sig[t, pl.ds(row, 8), :] = acc[0]
            cur_e[t, pl.ds(row, 8), :] = acc[1]
            cur_n[t, pl.ds(row + 8, 8), :] = acc[2]

    def both(lo, hi):
        @pl.loop(lo, hi)
        def _(c):
            columns(c)

    both(0, 1)
    both(n_rt - 1, n_rt)
    n_up = rcopy(cur_n.at[:, 8:16], cur_n.at[:, rows + 8 : rows + 16], 0, up)
    n_dn = rcopy(cur_n.at[:, rows : rows + 8], cur_n.at[:, 0:8], 1, dn)
    i_up = rcopy(ion.at[:, :, 8:16], ion.at[:, :, rows + 8 : rows + 16], 2, up)
    i_dn = rcopy(ion.at[:, :, rows : rows + 8], ion.at[:, :, 0:8], 3, dn)
    i_lf = rcopy(ion.at[:, 0, 8 : 8 + rows], ion_fr, 4, lf)
    i_rt = rcopy(ion.at[:, lt - 1, 8 : 8 + rows], ion_fl, 5, rt)

    for s in range(3):
        for t in range(lt):
            ion_copy(s, t).wait()

    @pl.when(has_up)
    def _():
        n_up.start()
        i_up.start()

    @pl.when(has_dn)
    def _():
        n_dn.start()
        i_dn.start()

    @pl.when(jnp.logical_not(has_up))
    def _():
        cur_n[:, 0:8, :] = jnp.zeros((lt, 8, 128), F32)
        ion[:, :, 0:8, :] = jnp.zeros((3, lt, 8, 128), F32)

    @pl.when(jnp.logical_not(has_dn))
    def _():
        cur_n[:, rows + 8 : rows + 16, :] = jnp.zeros((lt, 8, 128), F32)
        ion[:, :, rows + 8 : rows + 16, :] = jnp.zeros((3, lt, 8, 128), F32)

    pieces = 4
    per = n_rt // pieces
    sig_copies = []
    for q in range(pieces):
        both(max(1, q * per), min(n_rt - 1, (q + 1) * per))
        band = slice(q * per * 8, (q + 1) * per * 8)
        copy = rcopy(sig.at[:, band], sig_rx.at[:, band], 6 + q, mirror)
        copy.start()
        sig_copies.append(copy)

    e_lf = rcopy(cur_e.at[0], e_fr, 10, lf)
    e_rt = rcopy(cur_e.at[lt - 1], e_fl, 11, rt)
    e_lf.start()
    e_rt.start()
    i_lf.start()
    i_rt.start()

    @pl.when(has_dn)
    def _():
        n_up.wait_recv()

    @pl.when(has_up)
    def _():
        n_dn.wait_recv()

    e_lf.wait_recv()
    e_rt.wait_recv()

    t_copies = []
    for q in range(pieces):
        @pl.loop(q * per, (q + 1) * per)
        def _(c):
            row = pl.multiple_of(8 * c, 8)
            tiles = [cur_e[t, pl.ds(row, 8), :] for t in range(lt)]
            tiles.append(jnp.where(lane < 64, e_fr[pl.ds(row, 8), :], e_fl[pl.ds(row, 8), :]))
            left, right = shifts(tiles)
            for t in range(lt):
                d_lon = 0.5 * (right[t] - left[t])
                d_lat = 0.5 * (cur_n[t, pl.ds(row + 9, 8), :] - cur_n[t, pl.ds(row + 7, 8), :])
                s_one[t, pl.ds(row, 8), :] = d_lon + d_lat
                t_out[t, pl.ds(row, 8), :] = d_lon - d_lat

        band = slice(q * per * 8, (q + 1) * per * 8)
        copy = rcopy(t_out.at[:, band], t_rx.at[:, band], 12 + q, mirror)
        copy.start()
        t_copies.append(copy)

    def zero_rows(ref, lo, hi):
        ref[0:lt, lo:hi, :] = jnp.zeros((lt, hi - lo, 128), F32)

    @pl.when(jnp.logical_not(has_up))
    def _():
        zero_rows(S, 0, HALO)
        zero_rows(src, 0, HALO)

    @pl.when(jnp.logical_not(has_dn))
    def _():
        zero_rows(S, HALO + rows, 2 * HALO + rows)
        zero_rows(src, HALO + rows, 2 * HALO + rows)

    def combine(own, rx, out, q):
        @pl.loop((pieces - 1 - q) * per, (pieces - q) * per)
        def _(c):
            row = pl.multiple_of(8 * c, 8)
            back = pl.multiple_of(rows - 8 - 8 * c, 8)
            for t in range(lt):
                out[t, pl.ds(row + HALO, 8), :] = own[t, pl.ds(row, 8), :] + rev8(
                    rx[t, pl.ds(back, 8), :]
                )

    for q in range(pieces):
        sig_copies[q].wait_recv()
        combine(sig, sig_rx, S, q)
    for q in range(pieces):
        t_copies[q].wait_recv()
        combine(s_one, t_rx, src, q)

    lo_in, lo_out = slice(HALO, 2 * HALO), slice(0, HALO)
    hi_in, hi_out = slice(rows, rows + HALO), slice(rows + HALO, rows + 2 * HALO)
    mid = slice(HALO, HALO + rows)
    ups = [
        rcopy(f.at[0:lt, lo_in], f.at[0:lt, hi_out], 16 + k, up) for k, f in enumerate((S, src))
    ]
    dns = [
        rcopy(f.at[0:lt, hi_in], f.at[0:lt, lo_out], 18 + k, dn) for k, f in enumerate((S, src))
    ]

    @pl.when(has_up)
    def _():
        for c in ups:
            c.start()

    @pl.when(has_dn)
    def _():
        for c in dns:
            c.start()

    def pack(lo, hi):
        @pl.loop(lo // 8, hi // 8)
        def _(c):
            at = pl.ds(pl.multiple_of(8 * c, 8), 8)
            pk_l[at, :] = jnp.where(lane < 64, S[0, at, :], pltpu.roll(src[0, at, :], 64, 1))
            pk_r[at, :] = jnp.where(
                lane >= 64, S[lt - 1, at, :], pltpu.roll(src[lt - 1, at, :], 64, 1)
            )

    lons = []

    def send_lon(part, k):
        lons.append(rcopy(pk_l.at[part], rx_fr.at[part], k, lf))
        lons.append(rcopy(pk_r.at[part], rx_fl.at[part], k + 1, rt))
        lons[-2].start()
        lons[-1].start()

    pack(HALO, HALO + rows)
    send_lon(mid, 20)

    @pl.when(has_up)
    def _():
        for c in dns:
            c.wait_recv()

    pack(0, HALO)
    send_lon(lo_out, 22)

    @pl.when(has_dn)
    def _():
        for c in ups:
            c.wait_recv()

    pack(HALO + rows, 2 * HALO + rows)
    send_lon(hi_out, 24)
    for c in lons:
        c.wait_recv()

    n_ext = (rows + 2 * HALO) // 8
    total = rows * nlat

    @pl.loop(0, n_ext)
    def _(c):
        at = pl.ds(pl.multiple_of(8 * c, 8), 8)
        fr, fl = rx_fr[at, :], rx_fl[at, :]
        s_halo = jnp.where(lane < 64, fr, fl)
        S[lt, at, :] = s_halo
        src[lt, at, :] = pltpu.roll(jnp.where(lane >= 64, fr, fl), 64, 1)
        tiles = [S[t, at, :] for t in range(lt)] + [s_halo]
        for t, v in enumerate(smooth(tiles)):
            u[t, at, :] = v
            w[t, at, :] = jnp.zeros((8, 128), F32)

    theta = 0.5 * (HIGH_BOUND + LOW_BOUND)

    def column_conv(ref, t, row):
        return (
            ref[t, pl.ds(row - 1, 8), :] + ref[t, pl.ds(row + 1, 8), :]
        ) + 2.0 * ref[t, pl.ds(row, 8), :]

    @pl.loop(1, n_ext - 1)
    def _(c):
        row = pl.multiple_of(8 * c, 8)
        at = pl.ds(row, 8)
        where = sub + (row - HALO + me_lat * rows)
        inside = (where >= 0) & (where < total)
        for t in range(nt):
            s = S[t, at, :]
            diag = DAMPING + 0.5 * (4.0 * s + column_conv(u, t, row))
            inv = jnp.where(inside, 1.0 / diag, 0.0)
            half = 0.5 * inv
            r[t, at, :] = half
            g[t, at, :] = half * s
            first = src[t, at, :] * inv
            sp[t, at, :] = first
            d[t, at, :] = first * (1.0 / theta)
            x[t, at, :] = jnp.zeros((8, 128), F32)

    def sweep(k, lo, hi):
        c1 = coef[0, k]
        c2 = coef[1, k]

        @pl.loop(lo, hi, unroll=2)
        def _(c):
            at = pl.ds(pl.multiple_of(8 * c, 8), 8)
            xs = [x[t, at, :] + d[t, at, :] for t in range(nt)]
            ys = [S[t, at, :] * xs[t] for t in range(nt)]
            us = smooth(xs)
            ws = smooth(ys)
            for t in range(nt):
                x[t, at, :] = xs[t]
                u[t, at, :] = us[t]
                w[t, at, :] = ws[t]

        @pl.loop(lo, hi, unroll=2)
        def _(c):
            row = pl.multiple_of(8 * c, 8)
            at = pl.ds(row, 8)
            for t in range(nt):
                gg = g[t, at, :]
                xx = x[t, at, :]
                z = (sp[t, at, :] - xx) + (
                    gg * (column_conv(u, t, row) - 4.0 * xx)
                    + r[t, at, :] * column_conv(w, t, row)
                )
                d[t, at, :] = c1 * d[t, at, :] + c2 * z

    half = SWEEPS // 2

    @pl.loop(0, half)
    def _(k):
        sweep(k, 1, n_ext - 1)

    @pl.loop(half, SWEEPS - 1)
    def _(k):
        sweep(k, 2, n_ext - 2)

    @pl.loop(2, n_ext - 2)
    def _(c):
        at = pl.ds(pl.multiple_of(8 * c, 8), 8)
        for t in range(nt):
            x[t, at, :] = x[t, at, :] + d[t, at, :]

    pot_copies = [
        pltpu.make_async_copy(
            x.at[t, HALO : HALO + rows], pot_h.at[:, t * 128 : (t + 1) * 128], sem_out.at[0, t]
        )
        for t in range(lt)
    ]
    for c in pot_copies:
        c.start()

    @pl.when(has_dn)
    def _():
        i_up.wait_recv()

    @pl.when(has_up)
    def _():
        i_dn.wait_recv()

    i_lf.wait_recv()
    i_rt.wait_recv()

    def drift(c):
        row = pl.multiple_of(8 * c, 8)
        at = pl.ds(row + HALO, 8)
        left, right = shifts([x[t, at, :] for t in range(nt)])
        de = [
            -0.5 * (x[t, pl.ds(row + HALO + 1, 8), :] - x[t, pl.ds(row + HALO - 1, 8), :])
            for t in range(lt)
        ]
        dn_ = [0.5 * (right[t] - left[t]) for t in range(lt)]
        return row, de, dn_

    mx[...] = jnp.zeros((8, 128), F32)

    @pl.loop(0, n_rt)
    def _(c):
        row, de, dn_ = drift(c)
        best = mx[...]
        for t in range(lt):
            best = jnp.maximum(best, jnp.abs(de[t]) + jnp.abs(dn_[t]))
        mx[...] = best

    lat_copies = []
    for o in range(1, nlat):
        lat_copies.append(
            pltpu.make_async_remote_copy(
                src_ref=mx, dst_ref=rx_lat.at[o - 1],
                send_sem=ss_lat.at[o - 1], recv_sem=rs_lat.at[o - 1],
                device_id=(lax.rem(me_lat + o, nlat), me_lon), device_id_type=MESH,
            )
        )
        lat_copies[-1].start()

    def fluxes(s, lo, hi):
        @pl.loop(lo, hi)
        def _(c):
            row, de, dn_ = drift(c)
            at = pl.ds(row + 8, 8)
            tiles = [ion[s, t, at, :] for t in range(lt)]
            tiles.append(
                jnp.where(lane < 64, ion_fr[s, pl.ds(row, 8), :], ion_fl[s, pl.ds(row, 8), :])
            )
            left, right = shifts(tiles)
            for t in range(lt):
                n = tiles[t]
                f = jnp.maximum(de[t], 0.0) * (n - left[t])
                f = f + jnp.minimum(de[t], 0.0) * (right[t] - n)
                f = f + jnp.maximum(dn_[t], 0.0) * (n - ion[s, t, pl.ds(row + 7, 8), :])
                f = f + jnp.minimum(dn_[t], 0.0) * (ion[s, t, pl.ds(row + 9, 8), :] - n)
                flux[s, t, pl.ds(row, 8), :] = f

    fluxes(0, 0, n_rt)
    fluxes(1, 0, n_rt)
    best = mx[...]
    for o in range(1, nlat):
        lat_copies[o - 1].wait_recv()
        best = jnp.maximum(best, rx_lat[o - 1])
    mx2[...] = best
    lon_copies = []
    for o in range(1, nlon):
        lon_copies.append(
            pltpu.make_async_remote_copy(
                src_ref=mx2, dst_ref=rx_lon.at[o - 1],
                send_sem=ss_lon.at[o - 1], recv_sem=rs_lon.at[o - 1],
                device_id=(me_lat, lax.rem(me_lon + o, nlon)), device_id_type=MESH,
            )
        )
        lon_copies[-1].start()
    fluxes(2, 0, n_rt)
    best = mx2[...]
    for o in range(1, nlon):
        lon_copies[o - 1].wait_recv()
        best = jnp.maximum(best, rx_lon[o - 1])
    best = jnp.max(best, axis=0, keepdims=True)
    best = jnp.max(best, axis=1, keepdims=True)
    step = jnp.broadcast_to(COURANT / (best + 1e-6), (8, 128))

    upd_copies = []
    for s in range(3):
        scale = MOBILITY[s] * step

        @pl.loop(0, n_rt)
        def _(c):
            row = pl.multiple_of(8 * c, 8)
            for t in range(lt):
                upd[s, t, pl.ds(row, 8), :] = (
                    ion[s, t, pl.ds(row + 8, 8), :] - scale * flux[s, t, pl.ds(row, 8), :]
                )

        for t in range(lt):
            c = pltpu.make_async_copy(
                upd.at[s, t], upd_h.at[s, :, t * 128 : (t + 1) * 128], sem_out.at[1 + s, t]
            )
            c.start()
            upd_copies.append(c)

    @pl.when(has_up)
    def _():
        for c in [n_up, i_up] + ups:
            c.wait_send()

    @pl.when(has_dn)
    def _():
        for c in [n_dn, i_dn] + dns:
            c.wait_send()

    for c in [i_lf, i_rt, e_lf, e_rt] + sig_copies + t_copies + lons + lat_copies + lon_copies:
        c.wait_send()
    for c in pot_copies + upd_copies:
        c.wait()


def solution(mesh):
    nlat, nlon = mesh.shape["lat"], mesh.shape["lon"]
    theta, first_list, second_list = chebyshev_factors()

    def shards(pedersen, hall_conductivity, east_wind, north_wind, ion_density):
        lev, rows, cols = pedersen.shape
        lt = cols // 128
        nt = lt + 1
        ext = rows + 2 * HALO
        vm = lambda *shape: pltpu.VMEM(shape, F32)
        dma = lambda *shape: pltpu.SemaphoreType.DMA(shape)
        coef = jnp.array([first_list, second_list], F32)
        anyspec = pl.BlockSpec(memory_space=pl.ANY)
        return pl.pallas_call(
            functools.partial(kernel, nlat, nlon, lev, rows, lt),
            out_shape=(
                jax.ShapeDtypeStruct((rows, cols), F32),
                jax.ShapeDtypeStruct((3, rows, cols), F32),
            ),
            in_specs=[pl.BlockSpec(memory_space=pltpu.SMEM)] + [anyspec] * 5,
            out_specs=(anyspec, anyspec),
            scratch_shapes=[vm(lev, rows, cols)] * 4
            + [vm(3, lt, rows + 16, 128), vm(3, rows, 128), vm(3, rows, 128)]
            + [vm(lt, rows, 128), vm(lt, rows, 128), vm(lt, rows + 16, 128)]
            + [vm(rows, 128)] * 2
            + [vm(lt, rows, 128)] * 4
            + [vm(nt, ext, 128)] * 2
            + [vm(ext, 128)] * 4
            + [vm(nt, ext, 128)] * 7
            + [vm(3, lt, rows, 128)] * 2
            + [vm(8, 128), vm(nlat - 1, 8, 128), vm(8, 128), vm(nlon - 1, 8, 128)]
            + [dma(rows // 8, 4), dma(3, lt), dma(4, lt), dma(26), dma(26)]
            + [dma(nlat - 1)] * 2
            + [dma(nlon - 1)] * 2,
            compiler_params=pltpu.CompilerParams(
                collective_id=0, has_side_effects=True, vmem_limit_bytes=60 * 1024 * 1024
            ),
        )(coef, pedersen, hall_conductivity, east_wind, north_wind, ion_density)

    spec = P(None, "lat", "lon")
    return jax.shard_map(
        shards,
        mesh=mesh,
        in_specs=(spec,) * 5,
        out_specs=(P("lat", "lon"), spec),
        check_vma=False,
    )
```

time: 443 us -> 80.4 us (0.18)
  waiting for transfers between devices: 209 us -> 0 us
  other arithmetic: 105 us -> 0 us
  Pallas kernels: 0 us -> 75.8 us
  starting transfers between devices: 62.4 us -> 0 us
  blocking collectives: 38.6 us -> 0 us
  local copies, waits for them, and re-layouts: 24.3 us -> 3.73 us
    ppermute x75 -> x0, waiting for transfers between devices: 209 us -> none  [the longest x36 103 us: padded(): before = lax.ppermute(last, axis, up)]
    pallas_call x0 -> x1, Pallas kernels: none -> 75.8 us  [shards(): pl.pallas_call(functools.partial(kernel, nlat, nlon, lev, rows, lt), out_...]
    ppermute x75 -> x0, starting transfers between devices: 62.4 us -> none  [the longest x36 33.3 us: padded(): after = lax.ppermute(initial, axis, down)]
    pmax x1 -> x0, blocking collectives: 38.6 us -> none  [shards(): lax.pmax(jnp.max(jnp.abs(drift_east) + jnp.abs(drift_north)), ('lat', 'lo...]
    add x18 -> x0, other arithmetic: 29.7 us -> none  [the longest x16 27.9 us: group(): first_table[position] * update_ext + second_table[position] * scaled]
    sub x16 -> x0, other arithmetic: 26.5 us -> none  [apply_operator(): result - weights[index_pair] * window(field_ext, shift_lat, shift_lon)]
    dynamic_slice x32 -> x0, local copies, waits for them, and re-layouts: 19.9 us -> none  [the longest x16 10.6 us: group(): first_table[position] * update_ext + second_table[position] * scaled]
    concatenate x16 -> x0, other arithmetic: 19.4 us -> none  [padded(): array = jnp.concatenate([before, array, after], axis=dim)]
  transfers between devices with their start and end apart: 75 -> 0, of which waited for: 73 -> 0; matrix products, arithmetic and copies ran while one was open for 5% -> 0% of each run, Pallas kernels for 0% -> 0%
where the time goes in v1:
time: 80.4 us; the launch traced here: 80.2 us
  Pallas kernels  75.8 us (94%)
  local copies, waits for them, and re-layouts  3.73 us (5%)
    pallas_call x1, Pallas kernels, shards(): pl.pallas_call(functools.partial(kernel, nlat, nlon, lev, rows, lt), out_...  75.8 us
    unnamed x2, local copies, waits for them, and re-layouts  3.73 us

profile of v1, /device:TPU:0, one launch (start us, length us, event | category | flops | bytes accessed | tf_op | source)
XLA Modules:
  0.0 80.2 jit_solution(8293225691025157641)
XLA Ops:
  0.6 75.8 %shard_map.77 = (f32[128,512]{1,0:T(8,128)}, f32[3,128,512]{2,1,0:T(8,128)}) custom-call(f32[2,16]{1,0:T(2,128)} %constant.2.clone.coef, f32[16,128,512]{2,1,0:T(8,128)} %ped_h.1, f32[16,128,512]{2,1,0:T(8,128)} %hall_h.1, f32[16,128,512]{2,1,0:T(8,128)} %east_h.1, f32[16,128,512]{2,1,0:T(8,128)} %north_h.1, f32[3,128,512]{2,1,0:T(8,128)} %ion_h.1), custom_call_target="tpu_custom_call" | custom-call | tf_op jit(solution)/shard_map/pallas_call | solution.py:541
  76.4 1.7 %copy.10 = f32[128,512]{1,0:T(8,128)} copy(f32[128,512]{1,0:T(8,128)} %get-tuple-element.4) | data formatting | bytes 524288
  78.1 2.1 %copy.11 = f32[3,128,512]{2,1,0:T(8,128)} copy(f32[3,128,512]{2,1,0:T(8,128)} %get-tuple-element.5) | data formatting | bytes 1572864

commit v2 on v1

--- a/solution.py
+++ b/solution.py
@@ -33,17 +33,21 @@
     return (theta, first_list, second_list)
 
 
+def unroll_of(count):
+    return max(k for k in range(1, 11) if count % k == 0)
+
+
 def kernel(
     nlat, nlon, lev, rows, lt,
     coef, ped_h, hall_h, east_h, north_h, ion_h,
     pot_h, upd_h,
     ped, hall, east, north,
-    ion, ion_fr, ion_fl,
+    ion, ipk_l, ipk_r, ion_fr, ion_fl,
     sig, cur_e, cur_n, e_fr, e_fl, s_one, t_out, sig_rx, t_rx,
     S, src, pk_l, pk_r, rx_fr, rx_fl,
     g, r, sp, x, d, u, w,
-    flux, upd, mx, rx_lat, mx2, rx_lon,
-    sem_in, sem_ion, sem_out, ss, rs, ss_lat, rs_lat, ss_lon, rs_lon,
+    flux, mx, rx_lat, mx2, rx_lon,
+    sem_in, sem_ion, ss, rs, ss_lat, rs_lat, ss_lon, rs_lon,
 ):
     n_rt = rows // 8
     nt = lt + 1
@@ -147,8 +151,8 @@
     n_dn = rcopy(cur_n.at[:, rows : rows + 8], cur_n.at[:, 0:8], 1, dn)
     i_up = rcopy(ion.at[:, :, 8:16], ion.at[:, :, rows + 8 : rows + 16], 2, up)
     i_dn = rcopy(ion.at[:, :, rows : rows + 8], ion.at[:, :, 0:8], 3, dn)
-    i_lf = rcopy(ion.at[:, 0, 8 : 8 + rows], ion_fr, 4, lf)
-    i_rt = rcopy(ion.at[:, lt - 1, 8 : 8 + rows], ion_fl, 5, rt)
+    i_lf = rcopy(ipk_l, ion_fr, 4, lf)
+    i_rt = rcopy(ipk_r, ion_fl, 5, rt)
 
     for s in range(3):
         for t in range(lt):
@@ -188,6 +192,19 @@
     e_rt = rcopy(cur_e.at[lt - 1], e_fl, 11, rt)
     e_lf.start()
     e_rt.start()
+
+    @pl.loop(0, n_rt)
+    def _(c):
+        at = pl.ds(pl.multiple_of(8 * c, 8), 8)
+        inner = pl.ds(pl.multiple_of(8 * c + 8, 8), 8)
+        a, b = [], []
+        for s in range(3):
+            v, q = ion[s, 0, inner, :], ion[s, lt - 1, inner, :]
+            a.append(pltpu.roll(v, 32 * s, 1) if s else v)
+            b.append(pltpu.roll(q, 32 * (s + 1), 1))
+        ipk_l[at, :] = jnp.where(lane < 32, a[0], jnp.where(lane < 64, a[1], a[2]))
+        ipk_r[at, :] = jnp.where(lane < 32, b[0], jnp.where(lane < 64, b[1], b[2]))
+
     i_lf.start()
     i_rt.start()
 
@@ -353,7 +370,7 @@
         c1 = coef[0, k]
         c2 = coef[1, k]
 
-        @pl.loop(lo, hi, unroll=2)
+        @pl.loop(lo, hi, unroll=unroll_of(hi - lo))
         def _(c):
             at = pl.ds(pl.multiple_of(8 * c, 8), 8)
             xs = [x[t, at, :] + d[t, at, :] for t in range(nt)]
@@ -365,7 +382,7 @@
                 u[t, at, :] = us[t]
                 w[t, at, :] = ws[t]
 
-        @pl.loop(lo, hi, unroll=2)
+        @pl.loop(lo, hi, unroll=unroll_of(hi - lo))
         def _(c):
             row = pl.multiple_of(8 * c, 8)
             at = pl.ds(row, 8)
@@ -394,14 +411,11 @@
         for t in range(nt):
             x[t, at, :] = x[t, at, :] + d[t, at, :]
 
-    pot_copies = [
-        pltpu.make_async_copy(
-            x.at[t, HALO : HALO + rows], pot_h.at[:, t * 128 : (t + 1) * 128], sem_out.at[0, t]
-        )
-        for t in range(lt)
-    ]
-    for c in pot_copies:
-        c.start()
+    @pl.loop(0, n_rt)
+    def _(c):
+        row = pl.multiple_of(8 * c, 8)
+        for t in range(lt):
+            pot_h[pl.ds(row, 8), t * 128 : (t + 1) * 128] = x[t, pl.ds(row + HALO, 8), :]
 
     @pl.when(has_dn)
     def _():
@@ -453,7 +467,11 @@
             at = pl.ds(row + 8, 8)
             tiles = [ion[s, t, at, :] for t in range(lt)]
             tiles.append(
-                jnp.where(lane < 64, ion_fr[s, pl.ds(row, 8), :], ion_fl[s, pl.ds(row, 8), :])
+                jnp.where(
+                    lane < 64,
+                    pltpu.roll(ion_fr[pl.ds(row, 8), :], (128 - 32 * s) % 128, 1),
+                    pltpu.roll(ion_fl[pl.ds(row, 8), :], 96 - 32 * s, 1),
+                )
             )
             left, right = shifts(tiles)
             for t in range(lt):
@@ -490,7 +508,6 @@
     best = jnp.max(best, axis=1, keepdims=True)
     step = jnp.broadcast_to(COURANT / (best + 1e-6), (8, 128))
 
-    upd_copies = []
     for s in range(3):
         scale = MOBILITY[s] * step
 
@@ -498,17 +515,10 @@
         def _(c):
             row = pl.multiple_of(8 * c, 8)
             for t in range(lt):
-                upd[s, t, pl.ds(row, 8), :] = (
+                upd_h[s, pl.ds(row, 8), t * 128 : (t + 1) * 128] = (
                     ion[s, t, pl.ds(row + 8, 8), :] - scale * flux[s, t, pl.ds(row, 8), :]
                 )
 
-        for t in range(lt):
-            c = pltpu.make_async_copy(
-                upd.at[s, t], upd_h.at[s, :, t * 128 : (t + 1) * 128], sem_out.at[1 + s, t]
-            )
-            c.start()
-            upd_copies.append(c)
-
     @pl.when(has_up)
     def _():
         for c in [n_up, i_up] + ups:
@@ -521,8 +531,6 @@
 
     for c in [i_lf, i_rt, e_lf, e_rt] + sig_copies + t_copies + lons + lat_copies + lon_copies:
         c.wait_send()
-    for c in pot_copies + upd_copies:
-        c.wait()
 
 
 def solution(mesh):
@@ -545,18 +553,18 @@
                 jax.ShapeDtypeStruct((3, rows, cols), F32),
             ),
             in_specs=[pl.BlockSpec(memory_space=pltpu.SMEM)] + [anyspec] * 5,
-            out_specs=(anyspec, anyspec),
+            out_specs=(pl.BlockSpec(memory_space=pltpu.VMEM),) * 2,
             scratch_shapes=[vm(lev, rows, cols)] * 4
-            + [vm(3, lt, rows + 16, 128), vm(3, rows, 128), vm(3, rows, 128)]
+            + [vm(3, lt, rows + 16, 128), vm(rows, 128), vm(rows, 128)] + [vm(rows, 128)] * 2
             + [vm(lt, rows, 128), vm(lt, rows, 128), vm(lt, rows + 16, 128)]
             + [vm(rows, 128)] * 2
             + [vm(lt, rows, 128)] * 4
             + [vm(nt, ext, 128)] * 2
             + [vm(ext, 128)] * 4
             + [vm(nt, ext, 128)] * 7
-            + [vm(3, lt, rows, 128)] * 2
+            + [vm(3, lt, rows, 128)]
             + [vm(8, 128), vm(nlat - 1, 8, 128), vm(8, 128), vm(nlon - 1, 8, 128)]
-            + [dma(rows // 8, 4), dma(3, lt), dma(4, lt), dma(26), dma(26)]
+            + [dma(rows // 8, 4), dma(3, lt), dma(26), dma(26)]
             + [dma(nlat - 1)] * 2
             + [dma(nlon - 1)] * 2,
             compiler_params=pltpu.CompilerParams(

time: 80.4 us -> 72.6 us (0.903)
  Pallas kernels: 75.8 us -> 67.8 us
    pallas_call x1, Pallas kernels: 75.8 us -> 67.8 us  [shards(): pl.pallas_call(functools.partial(kernel, nlat, nlon, lev, rows, lt), out_...]
where the time goes in v2:
time: 72.6 us; the launch traced here: 72.2 us
  Pallas kernels  67.8 us (93%)
  local copies, waits for them, and re-layouts  3.73 us (5%)
    pallas_call x1, Pallas kernels, shards(): pl.pallas_call(functools.partial(kernel, nlat, nlon, lev, rows, lt), out_...  67.8 us
    unnamed x2, local copies, waits for them, and re-layouts  3.73 us

profile of v2, /device:TPU:0, one launch (start us, length us, event | category | flops | bytes accessed | tf_op | source)
XLA Modules:
  0.0 72.2 jit_solution(5558697129536741459)
XLA Ops:
  0.6 67.8 %shard_map.77 = (f32[128,512]{1,0:T(8,128)}, f32[3,128,512]{2,1,0:T(8,128)}) custom-call(f32[2,16]{1,0:T(2,128)} %constant.2.clone.coef, f32[16,128,512]{2,1,0:T(8,128)} %ped_h.1, f32[16,128,512]{2,1,0:T(8,128)} %hall_h.1, f32[16,128,512]{2,1,0:T(8,128)} %east_h.1, f32[16,128,512]{2,1,0:T(8,128)} %north_h.1, f32[3,128,512]{2,1,0:T(8,128)} %ion_h.1), custom_call_target="tpu_custom_call" | custom-call | tf_op jit(solution)/shard_map/pallas_call | solution.py:549
  68.4 1.7 %copy.10 = f32[128,512]{1,0:T(8,128)} copy(f32[128,512]{1,0:T(8,128)} %get-tuple-element.4) | data formatting | bytes 524288
  70.1 2.1 %copy.11 = f32[3,128,512]{2,1,0:T(8,128)} copy(f32[3,128,512]{2,1,0:T(8,128)} %get-tuple-element.5) | data formatting | bytes 1572864

commit v3 on v2

--- a/solution.py
+++ b/solution.py
@@ -44,7 +44,7 @@
     ped, hall, east, north,
     ion, ipk_l, ipk_r, ion_fr, ion_fl,
     sig, cur_e, cur_n, e_fr, e_fl, s_one, t_out, sig_rx, t_rx,
-    S, src, pk_l, pk_r, rx_fr, rx_fl,
+    S, src, SS, lhs, to_strided, to_plain, xn, pk_l, pk_r, rx_fr, rx_fl,
     g, r, sp, x, d, u, w,
     flux, mx, rx_lat, mx2, rx_lon,
     sem_in, sem_ion, ss, rs, ss_lat, rs_lat, ss_lon, rs_lon,
@@ -113,10 +113,6 @@
         right = [jnp.where(lane == 127, b[(j + 1) % m], b[j]) for j in range(m)]
         return left, right
 
-    def smooth(v):
-        left, right = shifts(v)
-        return [t + 0.5 * (p + q) for t, p, q in zip(v, left, right)]
-
     def rev8(v):
         v = pltpu.roll(v, 4, 0)
         for b in (2, 1):
@@ -220,7 +216,7 @@
     e_rt.wait_recv()
 
     t_copies = []
-    for q in range(pieces):
+    for q in [0, pieces - 1] + list(range(1, pieces - 1)):
         @pl.loop(q * per, (q + 1) * per)
         def _(c):
             row = pl.multiple_of(8 * c, 8)
@@ -236,7 +232,36 @@
         band = slice(q * per * 8, (q + 1) * per * 8)
         copy = rcopy(t_out.at[:, band], t_rx.at[:, band], 12 + q, mirror)
         copy.start()
-        t_copies.append(copy)
+        t_copies.append((q, copy))
+
+    width = nt * 128
+
+    @pl.loop(0, width // 16)
+    def _(c):
+        row = lax.broadcasted_iota(jnp.int32, (16, 128), 0) + 16 * c
+        col = lax.broadcasted_iota(jnp.int32, (16, 128), 1)
+        for t in range(nt):
+            there = jnp.where(row == col * nt + t, 1.0, 0.0).astype(jnp.bfloat16)
+            for part in range(3):
+                at = pl.ds(pl.multiple_of(part * width + 16 * c, 16), 16)
+                to_strided[at, t * 128 : (t + 1) * 128] = there
+
+    for j in range(nt):
+        @pl.loop(0, 8)
+        def _(c):
+            row = lax.broadcasted_iota(jnp.int32, (16, 128), 0) + 16 * c
+            col = lax.broadcasted_iota(jnp.int32, (16, 128), 1)
+            for t in range(nt):
+                back = jnp.where(row * nt + j == col + t * 128, 1.0, 0.0).astype(jnp.bfloat16)
+                for part in range(3):
+                    at = pl.ds(pl.multiple_of(part * width + j * 128 + 16 * c, 16), 16)
+                    to_plain[at, t * 128 : (t + 1) * 128] = back
+
+    def split(v, at, t):
+        for part in range(3):
+            low = v.astype(jnp.bfloat16)
+            lhs[at, part * width + t * 128 : part * width + (t + 1) * 128] = low
+            v = v - low.astype(F32)
 
     def zero_rows(ref, lo, hi):
         ref[0:lt, lo:hi, :] = jnp.zeros((lt, hi - lo, 128), F32)
@@ -264,13 +289,8 @@
     for q in range(pieces):
         sig_copies[q].wait_recv()
         combine(sig, sig_rx, S, q)
-    for q in range(pieces):
-        t_copies[q].wait_recv()
-        combine(s_one, t_rx, src, q)
-
     lo_in, lo_out = slice(HALO, 2 * HALO), slice(0, HALO)
     hi_in, hi_out = slice(rows, rows + HALO), slice(rows + HALO, rows + 2 * HALO)
-    mid = slice(HALO, HALO + rows)
     ups = [
         rcopy(f.at[0:lt, lo_in], f.at[0:lt, hi_out], 16 + k, up) for k, f in enumerate((S, src))
     ]
@@ -278,16 +298,6 @@
         rcopy(f.at[0:lt, hi_in], f.at[0:lt, lo_out], 18 + k, dn) for k, f in enumerate((S, src))
     ]
 
-    @pl.when(has_up)
-    def _():
-        for c in ups:
-            c.start()
-
-    @pl.when(has_dn)
-    def _():
-        for c in dns:
-            c.start()
-
     def pack(lo, hi):
         @pl.loop(lo // 8, hi // 8)
         def _(c):
@@ -305,8 +315,23 @@
         lons[-2].start()
         lons[-1].start()
 
-    pack(HALO, HALO + rows)
-    send_lon(mid, 20)
+    for i, (q, copy) in enumerate(t_copies):
+        copy.wait_recv()
+        combine(s_one, t_rx, src, q)
+        if i == 1:
+            @pl.when(has_up)
+            def _():
+                for c in ups:
+                    c.start()
+
+            @pl.when(has_dn)
+            def _():
+                for c in dns:
+                    c.start()
+
+        lo = HALO + (pieces - 1 - q) * per * 8
+        pack(lo, lo + per * 8)
+        send_lon(slice(lo, lo + per * 8), 20 + 2 * i)
 
     @pl.when(has_up)
     def _():
@@ -314,7 +339,7 @@
             c.wait_recv()
 
     pack(0, HALO)
-    send_lon(lo_out, 22)
+    send_lon(lo_out, 28)
 
     @pl.when(has_dn)
     def _():
@@ -322,22 +347,44 @@
             c.wait_recv()
 
     pack(HALO + rows, 2 * HALO + rows)
-    send_lon(hi_out, 24)
+    send_lon(hi_out, 30)
     for c in lons:
         c.wait_recv()
 
     n_ext = (rows + 2 * HALO) // 8
     total = rows * nlat
 
+    lane16 = lax.broadcasted_iota(jnp.int32, (16, 128), 1)
+    ext = 8 * n_ext
+
+    @pl.loop(0, n_ext // 2)
+    def _(c):
+        row = pl.multiple_of(16 * c, 16)
+        at = pl.ds(row, 16)
+        at2 = pl.ds(pl.multiple_of(row + ext, 16), 16)
+        fr, fl = rx_fr[at, :], rx_fl[at, :]
+        for t in range(lt):
+            split(S[t, at, :], at, t)
+            split(src[t, at, :], at2, t)
+        split(jnp.where(lane16 < 64, fr, fl), at, lt)
+        split(pltpu.roll(jnp.where(lane16 >= 64, fr, fl), 64, 1), at2, lt)
+
+    for f, out in enumerate((SS, sp)):
+        moved = jnp.dot(
+            lhs[f * ext : (f + 1) * ext, :], to_strided[...], preferred_element_type=F32
+        )
+        for t in range(nt):
+            out[t, :, :] = moved[:, t * 128 : (t + 1) * 128]
+
+    def smooth_strided(v):
+        left = [pltpu.roll(v[-1], 1, 1)] + v[:-1]
+        right = v[1:] + [pltpu.roll(v[0], 127, 1)]
+        return [t + 0.5 * (p + q) for t, p, q in zip(v, left, right)]
+
     @pl.loop(0, n_ext)
     def _(c):
         at = pl.ds(pl.multiple_of(8 * c, 8), 8)
-        fr, fl = rx_fr[at, :], rx_fl[at, :]
-        s_halo = jnp.where(lane < 64, fr, fl)
-        S[lt, at, :] = s_halo
-        src[lt, at, :] = pltpu.roll(jnp.where(lane >= 64, fr, fl), 64, 1)
-        tiles = [S[t, at, :] for t in range(lt)] + [s_halo]
-        for t, v in enumerate(smooth(tiles)):
+        for t, v in enumerate(smooth_strided([SS[t, at, :] for t in range(nt)])):
             u[t, at, :] = v
             w[t, at, :] = jnp.zeros((8, 128), F32)
 
@@ -355,13 +402,13 @@
         where = sub + (row - HALO + me_lat * rows)
         inside = (where >= 0) & (where < total)
         for t in range(nt):
-            s = S[t, at, :]
+            s = SS[t, at, :]
             diag = DAMPING + 0.5 * (4.0 * s + column_conv(u, t, row))
             inv = jnp.where(inside, 1.0 / diag, 0.0)
             half = 0.5 * inv
             r[t, at, :] = half
             g[t, at, :] = half * s
-            first = src[t, at, :] * inv
+            first = sp[t, at, :] * inv
             sp[t, at, :] = first
             d[t, at, :] = first * (1.0 / theta)
             x[t, at, :] = jnp.zeros((8, 128), F32)
@@ -374,9 +421,9 @@
         def _(c):
             at = pl.ds(pl.multiple_of(8 * c, 8), 8)
             xs = [x[t, at, :] + d[t, at, :] for t in range(nt)]
-            ys = [S[t, at, :] * xs[t] for t in range(nt)]
-            us = smooth(xs)
-            ws = smooth(ys)
+            ys = [SS[t, at, :] * xs[t] for t in range(nt)]
+            us = smooth_strided(xs)
+            ws = smooth_strided(ys)
             for t in range(nt):
                 x[t, at, :] = xs[t]
                 u[t, at, :] = us[t]
@@ -405,17 +452,25 @@
     def _(k):
         sweep(k, 2, n_ext - 2)
 
-    @pl.loop(2, n_ext - 2)
-    def _(c):
-        at = pl.ds(pl.multiple_of(8 * c, 8), 8)
+    near = rows + 16
+    first_row = HALO - 8
+
+    @pl.loop(0, near // 16)
+    def _(c):
+        row = pl.multiple_of(16 * c, 16)
+        at = pl.ds(pl.multiple_of(row + first_row, 8), 16)
         for t in range(nt):
-            x[t, at, :] = x[t, at, :] + d[t, at, :]
+            split(x[t, at, :] + d[t, at, :], pl.ds(row, 16), t)
+
+    moved = jnp.dot(lhs[0:near, :], to_plain[...], preferred_element_type=F32)
+    for t in range(nt):
+        xn[t, first_row : first_row + near, :] = moved[:, t * 128 : (t + 1) * 128]
 
     @pl.loop(0, n_rt)
     def _(c):
         row = pl.multiple_of(8 * c, 8)
         for t in range(lt):
-            pot_h[pl.ds(row, 8), t * 128 : (t + 1) * 128] = x[t, pl.ds(row + HALO, 8), :]
+            pot_h[pl.ds(row, 8), t * 128 : (t + 1) * 128] = xn[t, pl.ds(row + HALO, 8), :]
 
     @pl.when(has_dn)
     def _():
@@ -431,9 +486,9 @@
     def drift(c):
         row = pl.multiple_of(8 * c, 8)
         at = pl.ds(row + HALO, 8)
-        left, right = shifts([x[t, at, :] for t in range(nt)])
+        left, right = shifts([xn[t, at, :] for t in range(nt)])
         de = [
-            -0.5 * (x[t, pl.ds(row + HALO + 1, 8), :] - x[t, pl.ds(row + HALO - 1, 8), :])
+            -0.5 * (xn[t, pl.ds(row + HALO + 1, 8), :] - xn[t, pl.ds(row + HALO - 1, 8), :])
             for t in range(lt)
         ]
         dn_ = [0.5 * (right[t] - left[t]) for t in range(lt)]
@@ -529,7 +584,7 @@
         for c in [n_dn, i_dn] + dns:
             c.wait_send()
 
-    for c in [i_lf, i_rt, e_lf, e_rt] + sig_copies + t_copies + lons + lat_copies + lon_copies:
+    for c in [i_lf, i_rt, e_lf, e_rt] + sig_copies + [c for _, c in t_copies] + lons + lat_copies + lon_copies:
         c.wait_send()
 
 
@@ -543,6 +598,7 @@
         nt = lt + 1
         ext = rows + 2 * HALO
         vm = lambda *shape: pltpu.VMEM(shape, F32)
+        half = lambda *shape: pltpu.VMEM(shape, jnp.bfloat16)
         dma = lambda *shape: pltpu.SemaphoreType.DMA(shape)
         coef = jnp.array([first_list, second_list], F32)
         anyspec = pl.BlockSpec(memory_space=pl.ANY)
@@ -559,12 +615,13 @@
             + [vm(lt, rows, 128), vm(lt, rows, 128), vm(lt, rows + 16, 128)]
             + [vm(rows, 128)] * 2
             + [vm(lt, rows, 128)] * 4
-            + [vm(nt, ext, 128)] * 2
+            + [vm(nt, ext, 128)] * 3
+            + [half(2 * ext, 3 * nt * 128)] + [half(3 * nt * 128, nt * 128)] * 2 + [vm(nt, ext, 128)]
             + [vm(ext, 128)] * 4
             + [vm(nt, ext, 128)] * 7
             + [vm(3, lt, rows, 128)]
             + [vm(8, 128), vm(nlat - 1, 8, 128), vm(8, 128), vm(nlon - 1, 8, 128)]
-            + [dma(rows // 8, 4), dma(3, lt), dma(26), dma(26)]
+            + [dma(rows // 8, 4), dma(3, lt), dma(32), dma(32)]
             + [dma(nlat - 1)] * 2
             + [dma(nlon - 1)] * 2,
             compiler_params=pltpu.CompilerParams(

time: 72.6 us -> 68.8 us (0.948)
  Pallas kernels: 67.8 us -> 64.2 us
    pallas_call x1, Pallas kernels: 67.8 us -> 64.2 us  [shards(): pl.pallas_call(functools.partial(kernel, nlat, nlon, lev, rows, lt), out_...]
where the time goes in v3:
time: 68.8 us; the launch traced here: 68.6 us
  Pallas kernels  64.2 us (93%)
  local copies, waits for them, and re-layouts  3.73 us (5%)
    pallas_call x1, Pallas kernels, shards(): pl.pallas_call(functools.partial(kernel, nlat, nlon, lev, rows, lt), out_...  64.2 us
    unnamed x2, local copies, waits for them, and re-layouts  3.73 us

profile of v3, /device:TPU:0, one launch (start us, length us, event | category | flops | bytes accessed | tf_op | source)
XLA Modules:
  0.0 68.6 jit_solution(1799432749953943196)
XLA Ops:
  0.6 64.2 %shard_map.77 = (f32[128,512]{1,0:T(8,128)}, f32[3,128,512]{2,1,0:T(8,128)}) custom-call(f32[2,16]{1,0:T(2,128)} %constant.2.clone.coef, f32[16,128,512]{2,1,0:T(8,128)} %ped_h.1, f32[16,128,512]{2,1,0:T(8,128)} %hall_h.1, f32[16,128,512]{2,1,0:T(8,128)} %east_h.1, f32[16,128,512]{2,1,0:T(8,128)} %north_h.1, f32[3,128,512]{2,1,0:T(8,128)} %ion_h.1), custom_call_target="tpu_custom_call" | custom-call | tf_op jit(solution)/shard_map/pallas_call | solution.py:605
  64.9 1.7 %copy.10 = f32[128,512]{1,0:T(8,128)} copy(f32[128,512]{1,0:T(8,128)} %get-tuple-element.4) | data formatting | bytes 524288
  66.5 2.1 %copy.11 = f32[3,128,512]{2,1,0:T(8,128)} copy(f32[3,128,512]{2,1,0:T(8,128)} %get-tuple-element.5) | data formatting | bytes 1572864

commit v4 on v3

--- a/solution.py
+++ b/solution.py
@@ -43,7 +43,7 @@
     pot_h, upd_h,
     ped, hall, east, north,
     ion, ipk_l, ipk_r, ion_fr, ion_fl,
-    sig, cur_e, cur_n, e_fr, e_fl, s_one, t_out, sig_rx, t_rx,
+    sig, cur_e, cur_n, epk_l, epk_r, e_rx_r, e_rx_l, e_fr, e_fl, s_one, t_out, sig_rx, t_rx,
     S, src, SS, lhs, to_strided, to_plain, xn, pk_l, pk_r, rx_fr, rx_fl,
     g, r, sp, x, d, u, w,
     flux, mx, rx_lat, mx2, rx_lon,
@@ -184,8 +184,19 @@
         copy.start()
         sig_copies.append(copy)
 
-    e_lf = rcopy(cur_e.at[0], e_fr, 10, lf)
-    e_rt = rcopy(cur_e.at[lt - 1], e_fl, 11, rt)
+    for o in range(n_rt // 8):
+        for t, skip, out in ((0, 0, epk_l), (lt - 1, 16, epk_r)):
+            acc = None
+            for k in range(8):
+                lo = 64 * o + 8 * k
+                v = cur_e[t, lo : lo + 8, :]
+                turn = (16 * k + skip) % 128
+                v = pltpu.roll(v, turn, 1) if turn else v
+                acc = v if k == 0 else jnp.where(lane < 16 * k, acc, v)
+            out[8 * o : 8 * o + 8, :] = acc
+
+    e_lf = rcopy(epk_l, e_rx_r, 10, lf)
+    e_rt = rcopy(epk_r, e_rx_l, 11, rt)
     e_lf.start()
     e_rt.start()
 
@@ -214,6 +225,13 @@
 
     e_lf.wait_recv()
     e_rt.wait_recv()
+    for o in range(n_rt // 8):
+        part = slice(8 * o, 8 * o + 8)
+        for k in range(8):
+            lo = 64 * o + 8 * k
+            v, q = e_rx_r[part, :], e_rx_l[part, :]
+            e_fr[lo : lo + 8, :] = pltpu.roll(v, 128 - 16 * k, 1) if k else v
+            e_fl[lo : lo + 8, :] = pltpu.roll(q, 112 - 16 * k, 1) if k < 7 else q
 
     t_copies = []
     for q in [0, pieces - 1] + list(range(1, pieces - 1)):
@@ -588,6 +606,17 @@
         c.wait_send()
 
 
+def write_out(pot_v, upd_v, pot_h, upd_h, sem):
+    copies = [
+        pltpu.make_async_copy(upd_v, upd_h, sem.at[1]),
+        pltpu.make_async_copy(pot_v, pot_h, sem.at[0]),
+    ]
+    for c in copies:
+        c.start()
+    for c in copies:
+        c.wait()
+
+
 def solution(mesh):
     nlat, nlon = mesh.shape["lat"], mesh.shape["lon"]
     theta, first_list, second_list = chebyshev_factors()
@@ -602,7 +631,7 @@
         dma = lambda *shape: pltpu.SemaphoreType.DMA(shape)
         coef = jnp.array([first_list, second_list], F32)
         anyspec = pl.BlockSpec(memory_space=pl.ANY)
-        return pl.pallas_call(
+        pot, upd = pl.pallas_call(
             functools.partial(kernel, nlat, nlon, lev, rows, lt),
             out_shape=(
                 jax.ShapeDtypeStruct((rows, cols), F32),
@@ -613,6 +642,7 @@
             scratch_shapes=[vm(lev, rows, cols)] * 4
             + [vm(3, lt, rows + 16, 128), vm(rows, 128), vm(rows, 128)] + [vm(rows, 128)] * 2
             + [vm(lt, rows, 128), vm(lt, rows, 128), vm(lt, rows + 16, 128)]
+            + [vm(rows // 8, 128)] * 4
             + [vm(rows, 128)] * 2
             + [vm(lt, rows, 128)] * 4
             + [vm(nt, ext, 128)] * 3
@@ -628,6 +658,16 @@
                 collective_id=0, has_side_effects=True, vmem_limit_bytes=60 * 1024 * 1024
             ),
         )(coef, pedersen, hall_conductivity, east_wind, north_wind, ion_density)
+        return pl.pallas_call(
+            write_out,
+            out_shape=(
+                jax.ShapeDtypeStruct((rows, cols), F32),
+                jax.ShapeDtypeStruct((3, rows, cols), F32),
+            ),
+            in_specs=[pl.BlockSpec(memory_space=pltpu.VMEM)] * 2,
+            out_specs=(anyspec, anyspec),
+            scratch_shapes=[dma(2)],
+        )(pot, upd)
 
     spec = P(None, "lat", "lon")
     return jax.shard_map(

time: 68.8 us -> 67.2 us (0.977)
  local copies, waits for them, and re-layouts: 3.73 us -> 0 us
  Pallas kernels: 64.2 us -> 66.4 us
    unnamed x2 -> x0, local copies, waits for them, and re-layouts: 3.73 us -> none
    pallas_call x0 -> x1, Pallas kernels: none -> 2.2 us  [shards(): pl.pallas_call(write_out, out_shape=(jax.ShapeDtypeStruct((rows, cols), F...]
where the time goes in v4:
time: 67.2 us; the launch traced here: 67.1 us
  Pallas kernels  66.4 us (99%)
    pallas_call x1, Pallas kernels, shards(): pl.pallas_call(functools.partial(kernel, nlat, nlon, lev, rows, lt), out_...  64.2 us
    pallas_call x1, Pallas kernels, shards(): pl.pallas_call(write_out, out_shape=(jax.ShapeDtypeStruct((rows, cols), F...  2.2 us

profile of v4, /device:TPU:0, one launch (start us, length us, event | category | flops | bytes accessed | tf_op | source)
XLA Modules:
  0.0 67.1 jit_solution(13081938455012882792)
XLA Ops:
  0.6 64.2 %shard_map.77 = (f32[128,512]{1,0:T(8,128)}, f32[3,128,512]{2,1,0:T(8,128)}) custom-call(f32[2,16]{1,0:T(2,128)} %constant.2.clone.coef, f32[16,128,512]{2,1,0:T(8,128)} %ped_h.1, f32[16,128,512]{2,1,0:T(8,128)} %hall_h.1, f32[16,128,512]{2,1,0:T(8,128)} %east_h.1, f32[16,128,512]{2,1,0:T(8,128)} %north_h.1, f32[3,128,512]{2,1,0:T(8,128)} %ion_h.1), custom_call_target="tpu_custom_call" | custom-call | tf_op jit(solution)/shard_map/pallas_call | solution.py:634
  64.9 2.2 %shard_map.78 = (f32[128,512]{1,0:T(8,128)}, f32[3,128,512]{2,1,0:T(8,128)}) custom-call(f32[128,512]{1,0:T(8,128)} %get-tuple-element.4.pot_v, f32[3,128,512]{2,1,0:T(8,128)} %get-tuple-element.5.upd_v), custom_call_target="tpu_custom_call" | custom-call | tf_op jit(solution)/shard_map/pallas_call | solution.py:661
